TPU v7x, 32 devices: a whole 2x2x4 slice. The times are simulated.
32 devices in a mesh: groups: 2 (over y), mem: 8 (over z, x), lat: 2 (over core).
Axes of the slice: x: 2, y: 2, z: 4, core: 2. Of those that a mesh axis runs over, the one named last changes fastest.
Arguments:
- ensemble: float32 [16, 6, 256, 512], P(('groups', 'mem'), None, 'lat'), parts along dimension 0, may hold values from -1.5 to 1.5
- forcing_table: float32 [8, 256, 512], P(None, 'lat'), may hold values from -3 to 3
- ancestors: int32 [16], P('groups'), parts along dimension 0, may hold values from 0 to 7
- selector: int32 [16], P(('groups', 'mem')), parts along dimension 0, may hold values from 0 to 7
Outputs:
- advanced: float32 [16, 6, 256, 512], P(('groups', 'mem'), None, 'lat'), parts along dimension 0
There are 2 independent parts, one for each index of `groups`. A program takes and returns all parts, laid end to end along the dimension named above; an argument that names none is the same for every part. Nothing has to cross between parts.
Inputs may be any that keep to these rules, and one draw needn't show every extreme that they name: `ancestors`: index of a member of the same ensemble; some parents are named by several slots, many by none. `selector`: index of a forcing pattern.
All inputs are finite; a program needn't handle non-finite values.
Results may differ from a plain program's by a relative error of at most 0.00002.
Values sent between devices are 32-bit elements; how exact they have to be, the bound alone decides.
No kernel may reach another device: no remote copies, remote signals or barrier semaphores. Data moves between devices by JAX's collectives and lax.ppermute only.
A program may use at most 192 MiB of HBM per device.

v0:
```python
import functools

import jax
import jax.numpy as jnp
from jax import lax
from jax.experimental import pallas as pl
from jax.experimental.pallas import tpu as pltpu
from jax.sharding import PartitionSpec as P

STEPS = 3


TIME_STEP = 0.25
DENSITY_RATIO = 0.9
DRAG_RATE = 0.1
CORIOLIS_MEAN = 0.5

TILE = 8
LANES = 128


def copy_members(block, ancestors):
    slots, fields_count, band_rows, columns = block.shape
    count = lax.axis_size("mem")
    pieces = block.reshape(count, slots * fields_count * band_rows // count, columns)
    spread = lax.all_to_all(pieces, "mem", split_axis=0, concat_axis=0, tiled=True)
    taken = jnp.take(spread, ancestors, axis=0, mode="clip")
    moved = lax.all_to_all(taken, "mem", split_axis=0, concat_axis=0, tiled=True)
    return moved.reshape(slots * fields_count, band_rows, columns)


def edge_rows(block):
    rows = block.shape[-2]
    dim = block.ndim - 2
    count = lax.axis_size("lat")
    place = lax.axis_index("lat")
    if count == 2:
        sent = lax.dynamic_slice_in_dim(block, (1 - place) * (rows - TILE), TILE, axis=dim)
        got = lax.ppermute(sent, "lat", [(0, 1), (1, 0)])
        return jnp.where(place > 0, got, 0.0), jnp.where(place < 1, got, 0.0)
    forward = [(i, i + 1) for i in range(count - 1)]
    backward = [(target, source) for source, target in forward]
    below = lax.ppermute(lax.slice_in_dim(block, rows - TILE, rows, axis=dim), "lat", forward)
    above = lax.ppermute(lax.slice_in_dim(block, 0, TILE, axis=dim), "lat", backward)
    return below, above


HEIGHT_SCALE = TIME_STEP * TIME_STEP / 2
SPEED_SCALE = TIME_STEP / 2


def stencil_kernel(count, place_ref, parent_ref, low_ref, high_ref, force_ref, force_low_ref, force_high_ref, out_ref, first, second, force):
    rows, columns = parent_ref.shape[1:]
    blocks = rows // TILE
    strips = columns // LANES
    place = place_ref[0]
    total = float(rows * count)
    tile = (TILE, LANES)
    sub = lax.broadcasted_iota(jnp.int32, tile, 0)
    lane = lax.broadcasted_iota(jnp.int32, tile, 1)
    bottom = sub == 0
    left = lane == 0
    right = lane == LANES - 1
    zero = jnp.zeros(tile, jnp.float32)
    head = 2 * TILE
    last = head + rows

    def scaled(field, value):
        return HEIGHT_SCALE + HEIGHT_SCALE * value if field % 3 == 0 else SPEED_SCALE * value

    for strip in range(strips):
        span = slice(strip * LANES, (strip + 1) * LANES)
        for field in range(6):
            low = scaled(field, low_ref[field, :, span])
            high = scaled(field, high_ref[field, :, span])
            for buffer in (first, second):
                buffer[field, strip, :TILE] = zero
                buffer[field, strip, last + TILE : last + 2 * TILE] = zero
                buffer[field, strip, last + 2 * TILE :] = zero
                buffer[field, strip, TILE:head] = low
                buffer[field, strip, last : last + TILE] = high
            first[field, strip, head:last] = scaled(field, parent_ref[field, :, span])
            if field % 3 == 2:
                edge = first[field, strip, head : head + TILE]
                first[field, strip, head : head + TILE] = jnp.where(sub + place > 0, edge, 0.0)
        force[strip, TILE:head] = (TIME_STEP * SPEED_SCALE) * force_low_ref[:, span]
        force[strip, head:last] = (TIME_STEP * SPEED_SCALE) * force_ref[:, span]
        force[strip, last : last + TILE] = (TIME_STEP * SPEED_SCALE) * force_high_ref[:, span]

    def west(values):
        turned = [pltpu.roll(value, 1, 1) for value in values]
        return [jnp.where(left, turned[i - 1], turned[i]) for i in range(strips)]

    def east(values):
        turned = [pltpu.roll(value, LANES - 1, 1) for value in values]
        return [jnp.where(right, turned[(i + 1) % strips], turned[i]) for i in range(strips)]

    def load(source, field, block, offset=0):
        return [source[field, strip, pl.ds(TILE * (block + 1) + offset, TILE)] for strip in range(strips)]

    def each(function, *lists):
        return [function(*items) for items in zip(*lists)]

    def keep(target, field, block, values):
        for strip in range(strips):
            target[field, strip, pl.ds(pl.multiple_of(TILE * (block + 1), TILE), TILE)] = values[strip]

    def give(field, block, values):
        for strip in range(strips):
            value = values[strip] * (1.0 / HEIGHT_SCALE) - 1.0 if field % 3 == 0 else values[strip] * (1.0 / SPEED_SCALE)
            out_ref[field, pl.ds(pl.multiple_of(TILE * (block - 1), TILE), TILE), strip * LANES : (strip + 1) * LANES] = value

    def heights(source, target, block):
        for base in (0, 3):
            thick = load(source, base, block)
            flux_x = each(lambda u, t, w: u * (t + w), load(source, base + 1, block), thick, west(thick))
            flux_y = each(lambda v, t, b: v * (t + b), load(source, base + 2, block), thick, load(source, base, block, -1))
            above_flux = each(lambda v, t, a: v * (t + a), load(source, base + 2, block, 1), thick, load(source, base, block, 1))
            new = each(lambda h, e, x, a, y: (h - (e - x)) - (a - y), thick, east(flux_x), flux_x, above_flux, flux_y)
            keep(target, base, block, new)

    def speeds(source, target, block, store):
        row = (sub + ((block - 1) * TILE + place * rows)).astype(jnp.float32)
        coriolis_u = (0.25 * TIME_STEP) * (CORIOLIS_MEAN + (row * (1.0 / total) - 0.5))
        coriolis_v = (0.25 * TIME_STEP) * (CORIOLIS_MEAN + ((row - 0.5) * (1.0 / total) - 0.5))
        upper, lower = load(target, 0, block), load(target, 3, block)
        below_upper, below_lower = load(target, 0, block, -1), load(target, 3, block, -1)
        for layer in range(2):
            base = 3 * layer
            if layer == 0:
                pressure = each(lambda a, b: a + b, upper, lower)
                below_pressure = each(lambda a, b: a + b, below_upper, below_lower)
            else:
                pressure = each(lambda a, b: DENSITY_RATIO * a + b, upper, lower)
                below_pressure = each(lambda a, b: DENSITY_RATIO * a + b, below_upper, below_lower)
            speed_u = load(source, base + 1, block)
            speed_v = load(source, base + 2, block)
            turn_v = each(lambda v, a: coriolis_u * (v + a), speed_v, load(source, base + 2, block, 1))
            if layer == 0:
                forced = [speed_u[strip] + force[strip, pl.ds(pl.multiple_of(TILE * (block + 1), TILE), TILE)] for strip in range(strips)]
            else:
                forced = [(1.0 - TIME_STEP * DRAG_RATE) * value for value in speed_u]
            pushed = west(each(lambda t, p: t + p, turn_v, pressure))
            store(base + 1, block, each(lambda f, t, p, w: (f + (t - p)) + w, forced, turn_v, pressure, pushed))
            sum_u = each(lambda u, b: u + b, speed_u, load(source, base + 1, block, -1))
            slope = each(lambda p, b: p - b, pressure, below_pressure)
            store(base + 2, block, each(lambda v, s, es, d: (v - coriolis_v * (s + es)) - d, speed_v, sum_u, east(sum_u), slope))

    start = jnp.where(place == 0, 1, 0)
    stop = jnp.where(place == count - 1, blocks + 1, blocks + 2)
    source, target = first, second
    for _ in range(STEPS - 1):
        heights(source, target, start)

        def step(block, carry, source=source, target=target):
            heights(source, target, block + 1)
            speeds(source, target, block, functools.partial(keep, target))
            return carry

        lax.fori_loop(start, stop, step, 0)

        @pl.when(place == 0)
        def _():
            for field in (2, 5):
                for strip in range(strips):
                    target[field, strip, head : head + TILE] = jnp.where(bottom, 0.0, target[field, strip, head : head + TILE])

        source, target = target, source
    heights(source, target, 0)
    heights(source, target, 1)

    def finish(block, carry):
        heights(source, target, block + 1)
        give(0, block, load(target, 0, block))
        give(3, block, load(target, 3, block))
        speeds(source, target, block, give)
        return carry

    lax.fori_loop(1, blocks + 1, finish, 0)

    @pl.when(place == 0)
    def _():
        for field in (2, 5):
            for strip in range(strips):
                span = slice(strip * LANES, (strip + 1) * LANES)
                out_ref[field, :TILE, span] = jnp.where(bottom, 0.0, out_ref[field, :TILE, span])


def stencil(place, parents, low, high, forcing, force_low, force_high):
    fields_count, rows, columns = parents.shape
    shape = (fields_count, columns // LANES, rows + 5 * TILE, LANES)
    vmem = pl.BlockSpec(memory_space=pltpu.VMEM)
    return pl.pallas_call(
        functools.partial(stencil_kernel, lax.axis_size("lat")),
        out_shape=jax.ShapeDtypeStruct(parents.shape, jnp.float32),
        in_specs=[pl.BlockSpec(memory_space=pltpu.SMEM)] + [vmem] * 6,
        out_specs=vmem,
        scratch_shapes=[pltpu.VMEM(shape, jnp.float32), pltpu.VMEM(shape, jnp.float32), pltpu.VMEM(shape[1:], jnp.float32)],
        compiler_params=pltpu.CompilerParams(vmem_limit_bytes=12 << 20),
        cost_estimate=pl.CostEstimate(flops=300 * rows * columns, bytes_accessed=52 * rows * columns, transcendentals=0),
    )(place, parents, low, high, forcing, force_low, force_high)


def on_device(ensemble, forcing_table, ancestors, selector):
    forcing = lax.dynamic_index_in_dim(forcing_table, selector[0], 0, keepdims=False)
    force_low, force_high = edge_rows(forcing)
    parents = copy_members(ensemble, ancestors)
    low, high = edge_rows(parents)
    place = lax.axis_index("lat").astype(jnp.int32)[None]
    result = stencil(place, parents, low, high, forcing, force_low, force_high)
    return result.reshape(ensemble.shape)


def solution(mesh):
    placed = (
        P(("groups", "mem"), None, "lat", None),
        P(None, "lat", None),
        P("groups"),
        P(("groups", "mem")),
    )
    return jax.shard_map(
        on_device,
        mesh=mesh,
        in_specs=placed,
        out_specs=P(("groups", "mem"), None, "lat", None),
        check_vma=False,
    )
```

profile of v0, /device:TPU:0, one launch (start us, length us, event | category | flops | bytes accessed | tf_op | source)
XLA Modules:
  0.0 101.8 jit_solution(14608739398620983389)
XLA Ops:
  0.0 0.0 copy-start
  0.0 0.0 copy-start.1
  0.0 7.4 %all-to-all-start = ((f32[8,96,512]{2,1,0:T(8,128)}), f32[8,96,512]{2,1,0:T(8,128)}, u32[]{:S(2)}, u32[]{:S(2)}) async-start(f32[8,96,512]{2,1,0:T(8,128)} %bitcast.12), calls=%async_computation | async-start | bytes 3145728 | tf_op jit(solution)/shard_map/all_to_all | solution.py:26
  7.4 0.0 copy-done.1
  7.4 37.1 %all-to-all-done = f32[8,96,512]{2,1,0:T(8,128)} async-done(((f32[8,96,512]{2,1,0:T(8,128)}), f32[8,96,512]{2,1,0:T(8,128)}, u32[]{:S(2)}, u32[]{:S(2)}) %all-to-all-start) | async-done | bytes 1572896 | tf_op jit(solution)/shard_map/all_to_all | solution.py:26
  44.5 3.2 %gather_fusion = f32[8,96,512]{2,1,0:T(8,128)} fusion(f32[8,96,512]{2,1,0:T(8,128)} %all-to-all-done, s32[1024]{0:T(1024)S(1)} %pad_clamp_fusion), kind=kCustom, calls=%fused_computation | custom fusion | bytes 3145760 | tf_op jit(solution)/shard_map/jit(_take)/gather | solution.py:27
  47.7 4.3 %all-to-all-start.1 = ((f32[8,96,512]{2,1,0:T(8,128)}), f32[8,96,512]{2,1,0:T(8,128)}, u32[]{:S(2)}, u32[]{:S(2)}) async-start(f32[8,96,512]{2,1,0:T(8,128)} %gather_fusion), calls=%async_computation.1 | async-start | bytes 3145728 | tf_op jit(solution)/shard_map/all_to_all | solution.py:28
  52.7 0.0 copy-done
  52.7 0.1 collective-permute-start.1
  52.8 35.8 %all-to-all-done.1 = f32[8,96,512]{2,1,0:T(8,128)} async-done(((f32[8,96,512]{2,1,0:T(8,128)}), f32[8,96,512]{2,1,0:T(8,128)}, u32[]{:S(2)}, u32[]{:S(2)}) %all-to-all-start.1) | async-done | bytes 1572896 | tf_op jit(solution)/shard_map/all_to_all | solution.py:28
  88.7 0.9 constant_dynamic-slice_fusion
  89.6 0.0 collective-permute-start
  89.6 0.0 collective-permute-done.1
  89.6 1.3 %collective-permute-done = f32[6,8,512]{2,1,0:T(8,128)S(1)} collective-permute-done((f32[6,8,512]{2,1,0:T(8,128)S(1)}, f32[6,8,512]{2,1,0:T(8,128)S(1)}, u32[]{:S(2)}, u32[]{:S(2)}) %collective-permute-start) | collective-permute-done | bytes 98336 | tf_op jit(solution)/shard_map/ppermute | solution.py:39
  90.9 10.9 %shard_map.46 = f32[6,128,512]{2,1,0:T(8,128)} custom-call(s32[1]{0:T(128)} %bitcast.place_ref, f32[6,128,512]{2,1,0:T(8,128)} %bitcast.2.parent_ref, f32[6,8,512]{2,1,0:T(8,128)S(1)} %get-tuple-element.6.low_ref, f32[6,8,512]{2,1,0:T(8,128)S(1)} %get-tuple-element.5.high_ref, f32[128,512]{1,0:T(8,128)S(1)} %dynamic-slice_bitcast_fusion.force_ref, ...), custom_call_target="tpu_custom_call" | custom-call | flops 19660800 | bytes 3407872 | tf_op jit(solution)/shard_map/pallas_call | solution.py:193
  (5 shorter events, 0.1 us)
Async XLA Ops:
  0.0 52.7 %copy-start = (f32[8,128,512]{2,1,0:T(8,128)S(1)}, f32[8,128,512]{2,1,0:T(8,128)}, u32[]{:S(2)}) copy-start(f32[8,128,512]{2,1,0:T(8,128)} %param.5) | copy-start | bytes 6291460
  0.0 7.4 %copy-start.1 = (s32[8]{0:T(128)S(1)}, s32[8]{0:T(128)}, u32[]{:S(2)}) copy-start(s32[8]{0:T(128)} %param.6) | copy-start | bytes 100
  0.0 44.5 %all-to-all-start = ((f32[8,96,512]{2,1,0:T(8,128)}), f32[8,96,512]{2,1,0:T(8,128)}, u32[]{:S(2)}, u32[]{:S(2)}) async-start(f32[8,96,512]{2,1,0:T(8,128)} %bitcast.12), calls=%async_computation | async-start | bytes 3145728 | tf_op jit(solution)/shard_map/all_to_all | solution.py:26
  47.7 40.9 %all-to-all-start.1 = ((f32[8,96,512]{2,1,0:T(8,128)}), f32[8,96,512]{2,1,0:T(8,128)}, u32[]{:S(2)}, u32[]{:S(2)}) async-start(f32[8,96,512]{2,1,0:T(8,128)} %gather_fusion), calls=%async_computation.1 | async-start | bytes 3145728 | tf_op jit(solution)/shard_map/all_to_all | solution.py:28
  52.7 36.9 %collective-permute-start.1 = (f32[8,512]{1,0:T(8,128)S(1)}, f32[8,512]{1,0:T(8,128)S(1)}, u32[]{:S(2)}, u32[]{:S(2)}) collective-permute-start(f32[8,512]{1,0:T(8,128)S(1)} %dynamic-slice_bitcast_fusion.1), channel_id=1, source_target_pairs={{0,1},{1,0},{2,3},{3,2},{4,5},{5,4},{6,7},{7,6},{8,9},{9,8},{10,11... | collective-permute-start | bytes 49160 | tf_op jit(solution)/shard_map/ppermute | solution.py:39
  89.6 1.3 %collective-permute-start = (f32[6,8,512]{2,1,0:T(8,128)S(1)}, f32[6,8,512]{2,1,0:T(8,128)S(1)}, u32[]{:S(2)}, u32[]{:S(2)}) collective-permute-start(f32[6,8,512]{2,1,0:T(8,128)S(1)} %constant_dynamic-slice_fusion), channel_id=1, source_target_pairs={{0,1},{1,0},{2,3},{3,2},{4,5},{5,4},{6,7},{7,6},{8,9},{9,8},{10,11... | collective-permute-start | bytes 294920 | tf_op jit(solution)/shard_map/ppermute | solution.py:39
where the time goes:
time: 102 us
  waiting for transfers between devices  74.2 us (73%)
  starting transfers between devices  11.8 us (12%)
  Pallas kernels  10.9 us (11%)
  local copies, waits for them, and re-layouts  4.14 us (4%)
    all_to_all x1, waiting for transfers between devices, copy_members(): lax.all_to_all(pieces, 'mem', split_axis=0, concat_axis=0, tiled=True)  37.1 us
    all_to_all x1, waiting for transfers between devices, copy_members(): lax.all_to_all(taken, 'mem', split_axis=0, concat_axis=0, tiled=True)  35.8 us
    pallas_call x1, Pallas kernels, stencil(): pl.pallas_call(functools.partial(stencil_kernel, lax.axis_size('lat')), o...  10.9 us
    all_to_all x1, starting transfers between devices, copy_members(): lax.all_to_all(pieces, 'mem', split_axis=0, concat_axis=0, tiled=True)  7.41 us
    all_to_all x1, starting transfers between devices, copy_members(): lax.all_to_all(taken, 'mem', split_axis=0, concat_axis=0, tiled=True)  4.29 us
    gather x1, local copies, waits for them, and re-layouts, copy_members(): taken = jnp.take(spread, ancestors, axis=0, mode='clip')  3.2 us
  transfers between devices with their start and end apart: 4, of which 3 were waited for; matrix products, arithmetic and copies ran while one was open for 1% of the time, Pallas kernels for 0%

commit v1 on v0

--- a/solution.py
+++ b/solution.py
@@ -19,38 +19,14 @@
 LANES = 128
 
 
-def copy_members(block, ancestors):
-    slots, fields_count, band_rows, columns = block.shape
-    count = lax.axis_size("mem")
-    pieces = block.reshape(count, slots * fields_count * band_rows // count, columns)
-    spread = lax.all_to_all(pieces, "mem", split_axis=0, concat_axis=0, tiled=True)
-    taken = jnp.take(spread, ancestors, axis=0, mode="clip")
-    moved = lax.all_to_all(taken, "mem", split_axis=0, concat_axis=0, tiled=True)
-    return moved.reshape(slots * fields_count, band_rows, columns)
-
-
-def edge_rows(block):
-    rows = block.shape[-2]
-    dim = block.ndim - 2
-    count = lax.axis_size("lat")
-    place = lax.axis_index("lat")
-    if count == 2:
-        sent = lax.dynamic_slice_in_dim(block, (1 - place) * (rows - TILE), TILE, axis=dim)
-        got = lax.ppermute(sent, "lat", [(0, 1), (1, 0)])
-        return jnp.where(place > 0, got, 0.0), jnp.where(place < 1, got, 0.0)
-    forward = [(i, i + 1) for i in range(count - 1)]
-    backward = [(target, source) for source, target in forward]
-    below = lax.ppermute(lax.slice_in_dim(block, rows - TILE, rows, axis=dim), "lat", forward)
-    above = lax.ppermute(lax.slice_in_dim(block, 0, TILE, axis=dim), "lat", backward)
-    return below, above
-
-
 HEIGHT_SCALE = TIME_STEP * TIME_STEP / 2
 SPEED_SCALE = TIME_STEP / 2
 
 
-def stencil_kernel(count, place_ref, parent_ref, low_ref, high_ref, force_ref, force_low_ref, force_high_ref, out_ref, first, second, force):
-    rows, columns = parent_ref.shape[1:]
+def stencil_kernel(count, pieces, place_ref, starts_ref, *refs):
+    parent_refs = refs[:pieces]
+    low_ref, high_ref, force_ref, force_low_ref, force_high_ref, out_ref, first, second, force = refs[pieces:]
+    rows, columns = force_ref.shape
     blocks = rows // TILE
     strips = columns // LANES
     place = place_ref[0]
@@ -71,15 +47,18 @@
     for strip in range(strips):
         span = slice(strip * LANES, (strip + 1) * LANES)
         for field in range(6):
-            low = scaled(field, low_ref[field, :, span])
-            high = scaled(field, high_ref[field, :, span])
+            low = scaled(field, jnp.where(place > 0, low_ref[field, :, span], 0.0))
+            high = scaled(field, jnp.where(place < count - 1, high_ref[field, :, span], 0.0))
             for buffer in (first, second):
                 buffer[field, strip, :TILE] = zero
                 buffer[field, strip, last + TILE : last + 2 * TILE] = zero
                 buffer[field, strip, last + 2 * TILE :] = zero
                 buffer[field, strip, TILE:head] = low
                 buffer[field, strip, last : last + TILE] = high
-            first[field, strip, head:last] = scaled(field, parent_ref[field, :, span])
+            for piece, parent_ref in enumerate(parent_refs):
+                height = parent_ref.shape[1]
+                here = pl.ds(pl.multiple_of(head + starts_ref[piece], TILE), height)
+                first[field, strip, here] = scaled(field, parent_ref[field, :, span])
             if field % 3 == 2:
                 edge = first[field, strip, head : head + TILE]
                 first[field, strip, head : head + TILE] = jnp.where(sub + place > 0, edge, 0.0)
@@ -186,28 +165,192 @@
                 out_ref[field, :TILE, span] = jnp.where(bottom, 0.0, out_ref[field, :TILE, span])
 
 
-def stencil(place, parents, low, high, forcing, force_low, force_high):
-    fields_count, rows, columns = parents.shape
+def stencil(parents, starts, edges, forcing, force_edges):
+    rows, columns = forcing.shape
+    fields_count = parents[0].shape[0]
     shape = (fields_count, columns // LANES, rows + 5 * TILE, LANES)
     vmem = pl.BlockSpec(memory_space=pltpu.VMEM)
+    smem = pl.BlockSpec(memory_space=pltpu.SMEM)
+    place = lax.axis_index("lat").astype(jnp.int32)[None]
     return pl.pallas_call(
-        functools.partial(stencil_kernel, lax.axis_size("lat")),
-        out_shape=jax.ShapeDtypeStruct(parents.shape, jnp.float32),
-        in_specs=[pl.BlockSpec(memory_space=pltpu.SMEM)] + [vmem] * 6,
+        functools.partial(stencil_kernel, lax.axis_size("lat"), len(parents)),
+        out_shape=jax.ShapeDtypeStruct((fields_count, rows, columns), jnp.float32),
+        in_specs=[smem] * 2 + [vmem] * (len(parents) + 5),
         out_specs=vmem,
         scratch_shapes=[pltpu.VMEM(shape, jnp.float32), pltpu.VMEM(shape, jnp.float32), pltpu.VMEM(shape[1:], jnp.float32)],
         compiler_params=pltpu.CompilerParams(vmem_limit_bytes=12 << 20),
         cost_estimate=pl.CostEstimate(flops=300 * rows * columns, bytes_accessed=52 * rows * columns, transcendentals=0),
-    )(place, parents, low, high, forcing, force_low, force_high)
+    )(place, starts, *parents, *edges, forcing, *force_edges)
+
+
+def edge_rows(block):
+    rows = block.shape[-2]
+    dim = block.ndim - 2
+    count = lax.axis_size("lat")
+    if count == 2:
+        sent = lax.dynamic_slice_in_dim(block, (1 - lax.axis_index("lat")) * (rows - TILE), TILE, axis=dim)
+        return swap_edges(sent)
+    forward = [(i, i + 1) for i in range(count - 1)]
+    backward = [(target, source) for source, target in forward]
+    below = lax.ppermute(lax.slice_in_dim(block, rows - TILE, rows, axis=dim), "lat", forward)
+    above = lax.ppermute(lax.slice_in_dim(block, 0, TILE, axis=dim), "lat", backward)
+    return below, above
+
+
+def swap_edges(sent):
+    got = lax.ppermute(sent, "lat", [(0, 1), (1, 0)])
+    return got, got
+
+
+def by_all_to_all(block, ancestors):
+    fields_count, band_rows, columns = block.shape
+    count = lax.axis_size("mem")
+    pieces = block.reshape(count, fields_count * band_rows // count, columns)
+    spread = lax.all_to_all(pieces, "mem", split_axis=0, concat_axis=0, tiled=True)
+    taken = jnp.take(spread, ancestors, axis=0, mode="clip")
+    moved = lax.all_to_all(taken, "mem", split_axis=0, concat_axis=0, tiled=True)
+    return moved.reshape(block.shape)
+
+
+PARTS = 4
+MEMBERS = 2 * PARTS
+CHUNKS = 2
+
+
+def shift(values, distance):
+    return lax.ppermute(values, "mem", [(i, i ^ distance) for i in range(MEMBERS)])
+
+
+def small_call(kernel, count, shape, scalars, arrays, held, scratch=()):
+    vmem = pl.BlockSpec(memory_space=pltpu.VMEM)
+    size = 4 * shape[0] * shape[1] * shape[2]
+    return pl.pallas_call(
+        kernel,
+        out_shape=[jax.ShapeDtypeStruct(shape, jnp.float32)] * count,
+        in_specs=[pl.BlockSpec(memory_space=pltpu.SMEM)] + [vmem] * held + [pl.BlockSpec(memory_space=pl.ANY)] * (len(arrays) - held),
+        out_specs=[vmem] * count,
+        scratch_shapes=list(scratch),
+        compiler_params=pltpu.CompilerParams(vmem_limit_bytes=4 << 20),
+        cost_estimate=pl.CostEstimate(flops=0, bytes_accessed=2 * count * size, transcendentals=0),
+    )(scalars, *arrays)
+
+
+def cut_kernel(starts_ref, block_ref, *refs):
+    outs, sem = refs[-PARTS - 1 : -1], refs[-1]
+    height = outs[0].shape[1]
+    copies = []
+    for k, out in enumerate(outs):
+        rows = pl.ds(pl.multiple_of(starts_ref[k], TILE), height)
+        copies.append(pltpu.make_async_copy(block_ref.at[:, rows, :], out, sem.at[k]))
+    for copy in copies:
+        copy.start()
+    for copy in copies:
+        copy.wait()
+
+
+def cut(block, starts, height, after):
+    shape = (block.shape[0], height, block.shape[2])
+    return small_call(cut_kernel, PARTS, shape, starts, [block, *after], 0, [pltpu.SemaphoreType.DMA((PARTS,))])
+
+
+def route_kernel(sources, count, chosen_ref, *refs):
+    for k, out in enumerate(refs[-count:]):
+        for j, source in enumerate(refs[:sources]):
+
+            @pl.when(chosen_ref[k] == j)
+            def _():
+                out[...] = source[...]
+
+
+def route(chosen, sources, count, after=()):
+    kernel = functools.partial(route_kernel, len(sources), count)
+    return small_call(kernel, count, sources[0].shape, chosen, [*sources, *after], len(sources))
+
+
+def edge_kernel(chosen_ref, *refs):
+    out = refs[-1]
+    for j, source in enumerate(refs[:-1]):
+
+        @pl.when(chosen_ref[0] == j)
+        def _():
+            out[...] = source[:, pl.ds(pl.multiple_of(chosen_ref[1], TILE), TILE), :]
+
+
+def crossings(ancestors):
+    ids = jnp.arange(MEMBERS, dtype=jnp.int32)
+    far = ids[:, None] // PARTS != ids[None, :] // PARTS
+    need = jnp.any((ancestors[:, None] == ids[None, :]) & far, axis=0)
+    ahead = need[:, None] & (ids[:, None] < ids[None, :]) & ~far
+    return need, jnp.sum(ahead.astype(jnp.int32), axis=0)
+
+
+def by_crossings(block, ancestors, finish):
+    fields_count, rows, columns = block.shape
+    ids = jnp.arange(MEMBERS, dtype=jnp.int32)
+    member = lax.axis_index("mem").astype(jnp.int32)
+    half, own = member // PARTS, member % PARTS
+    parts = own ^ jnp.arange(PARTS, dtype=jnp.int32)
+    span = rows // CHUNKS
+    height = span // PARTS
+    near = (lax.axis_index("lat") == 0).astype(jnp.int32)
+    starts = [((CHUNKS - 1 - c) * near + c * (1 - near)) * span + parts * height for c in range(CHUNKS)]
+
+    def spread(c, block, after):
+        held = cut(block, starts[c], height, after)
+        return [held[0]] + [shift(held[k], k) for k in range(1, PARTS)]
+
+    need, rank = crossings(ancestors)
+    most = jnp.max(rank + need.astype(jnp.int32))[None]
+    groups = lax.axis_size("groups")
+    for distance in range(1, groups):
+        other = lax.ppermute(most, "groups", [(i, (i + distance) % groups) for i in range(groups)])
+        most = jnp.maximum(most, other)
+    slots = half * PARTS + parts
+    parent = jnp.sum(jnp.where(slots[:, None] == ids[None, :], ancestors[None, :], 0), axis=1)
+    parent_rank = jnp.sum(jnp.where(parent[:, None] == ids[None, :], rank[None, :], 0), axis=1)
+    given_index = jnp.where(parent // PARTS == half, (parent % PARTS) ^ own, PARTS + parent_rank)
+
+    def plan(rounds, block, shared, need, rank, given_index, rest):
+        turns = jnp.arange(rounds, dtype=jnp.int32)
+        mine = need & (ids // PARTS == half)
+        order = jnp.sum(jnp.where(mine[None, :] & (rank[None, :] == turns[:, None]), ids[None, :] % PARTS, 0), axis=1)
+        crossed, final = (), []
+        for c in range(CHUNKS):
+            if c > 0:
+                shared = spread(c, block, shared[1:])
+            sent = route(order ^ own, shared, rounds, crossed)
+            crossed = [shift(part, PARTS) for part in sent]
+            given = route(given_index, [*shared, *crossed], PARTS)
+            final.append([given[0]] + [shift(given[k], k) for k in range(1, PARTS)])
+        return finish(final, starts, *rest)
+
+    return spread(0, block, ()), most, (need, rank, given_index), plan
 
 
 def on_device(ensemble, forcing_table, ancestors, selector):
+    rows = ensemble.shape[2]
+    block = ensemble.reshape(ensemble.shape[1:])
     forcing = lax.dynamic_index_in_dim(forcing_table, selector[0], 0, keepdims=False)
-    force_low, force_high = edge_rows(forcing)
-    parents = copy_members(ensemble, ancestors)
-    low, high = edge_rows(parents)
-    place = lax.axis_index("lat").astype(jnp.int32)[None]
-    result = stencil(place, parents, low, high, forcing, force_low, force_high)
+    force_edges = edge_rows(forcing)
+    fits = lax.axis_size("mem") == MEMBERS and lax.axis_size("lat") == 2 and rows % (CHUNKS * PARTS * TILE) == 0
+    if not fits:
+        parents = by_all_to_all(block, ancestors)
+        result = stencil([parents], jnp.zeros(1, jnp.int32), edge_rows(parents), forcing, force_edges)
+        return result.reshape(ensemble.shape)
+
+    def finish(final, starts, forcing, below, above):
+        height = final[0][0].shape[1]
+        own = lax.axis_index("mem").astype(jnp.int32) % PARTS
+        near = (lax.axis_index("lat") == 0).astype(jnp.int32)
+        chosen = jnp.stack([own ^ ((PARTS - 1) * near), (height - TILE) * near])
+        edge = small_call(edge_kernel, 1, (block.shape[0], TILE, block.shape[2]), chosen, final[0], PARTS)[0]
+        pieces = [piece for chunk in final for piece in chunk]
+        return stencil(pieces, jnp.concatenate(starts), swap_edges(edge), forcing, (below, above))
+
+    shared, most, tables, plan = by_crossings(block, ancestors, finish)
+    branches = [functools.partial(plan, rounds) for rounds in range(2, PARTS + 1)]
+    choice = jnp.clip(most[0] - 2, 0, PARTS - 2)
+    result = lax.switch(choice, branches, block, shared, *tables, (forcing, *force_edges))
     return result.reshape(ensemble.shape)
 
 

time: 102 us -> 103 us (level)
  waiting for transfers between devices: 74.2 us -> 48.9 us
  starting transfers between devices: 11.8 us -> 27.3 us
  Pallas kernels: 10.9 us -> 17.5 us
  other arithmetic: 0.03 us -> 3.6 us
  between operations: 0.75 us -> 2.05 us
  local copies, waits for them, and re-layouts: 4.14 us -> 2.94 us
    all_to_all x2 -> x0, waiting for transfers between devices: 72.9 us -> none  [the longest x1 37.1 us: copy_members(): lax.all_to_all(pieces, 'mem', split_axis=0, concat_axis=0, tiled=True)]
    ppermute x2 -> x21, waiting for transfers between devices: 1.27 us -> 48.9 us  [the longest x18 46.8 us: shift(): lax.ppermute(values, 'mem', [(i, i ^ distance) for i in range(MEMBERS)])]
    ppermute x2 -> x21, starting transfers between devices: 0.07 us -> 27.3 us  [the longest x18 25.3 us: shift(): lax.ppermute(values, 'mem', [(i, i ^ distance) for i in range(MEMBERS)])]
    all_to_all x2 -> x0, starting transfers between devices: 11.7 us -> none  [the longest x1 7.41 us: copy_members(): lax.all_to_all(pieces, 'mem', split_axis=0, concat_axis=0, tiled=True)]
    pallas_call x1 -> x8, Pallas kernels: 10.9 us -> 17.5 us  [the longest x1 8.83 us: stencil(): pl.pallas_call(functools.partial(stencil_kernel, lax.axis_size('lat'), le...]
    gather x1 -> x0, local copies, waits for them, and re-layouts: 3.2 us -> none  [copy_members(): taken = jnp.take(spread, ancestors, axis=0, mode='clip')]
    reduce_sum x0 -> x4, other arithmetic: none -> 1.23 us  [the longest x1 0.84 us: by_crossings(): jnp.sum(jnp.where(slots[:, None] == ids[None, :], ancestors[None, :], 0),...]
    unnamed x4 -> x2, local copies, waits for them, and re-layouts: 0.01 us -> 1.14 us
  transfers between devices with their start and end apart: 4 -> 21, of which waited for: 3 -> 12; matrix products, arithmetic and copies ran while one was open for 1% -> 5% of each run, Pallas kernels for 0% -> 4%
where the time goes in v1:
time: 103 us
  waiting for transfers between devices  48.9 us (47%)
  starting transfers between devices  27.3 us (27%)
  Pallas kernels  17.5 us (17%)
  other arithmetic  3.6 us (3%)
  local copies, waits for them, and re-layouts  2.94 us (3%)
  between operations  2.05 us (2%)
    ppermute x18, waiting for transfers between devices, shift(): lax.ppermute(values, 'mem', [(i, i ^ distance) for i in range(MEMBERS)])  46.8 us
    ppermute x18, starting transfers between devices, shift(): lax.ppermute(values, 'mem', [(i, i ^ distance) for i in range(MEMBERS)])  25.3 us
    pallas_call x1, Pallas kernels, stencil(): pl.pallas_call(functools.partial(stencil_kernel, lax.axis_size('lat'), le...  8.83 us
    pallas_call x7, Pallas kernels, small_call(): pl.pallas_call(kernel, out_shape=[jax.ShapeDtypeStruct(shape, jnp.float32...  8.66 us
  transfers between devices with their start and end apart: 21, of which 12 were waited for; matrix products, arithmetic and copies ran while one was open for 5% of the time, Pallas kernels for 4%

profile of v1, /device:TPU:0, one launch (start us, length us, event | category | flops | bytes accessed | tf_op | source)
XLA Modules:
  0.0 102.7 jit_solution(16739862593727238401)
XLA Ops:
  0.0 2.5 %shard_map.49 = (f32[6,16,512]{2,1,0:T(8,128)}, f32[6,16,512]{2,1,0:T(8,128)S(1)}, f32[6,16,512]{2,1,0:T(8,128)S(1)}, f32[6,16,512]{2,1,0:T(8,128)S(1)}) custom-call(s32[4]{0:T(128)S(1)} %broadcast_add_fusion.3.starts_ref, f32[6,128,512]{2,1,0:T(8,128)} %bitcast.27), custom_call_target="tpu_custom_call" | custom-call | bytes 1572864 | tf_op jit(solution)/shard_map/pallas_call | solution.py:227
  2.5 3.0 %collective-permute-start.49 = (f32[6,16,512]{2,1,0:T(8,128)S(1)}, f32[6,16,512]{2,1,0:T(8,128)S(1)}, u32[]{:S(2)}, u32[]{:S(2)}) collective-permute-start(f32[6,16,512]{2,1,0:T(8,128)S(1)} %get-tuple-element.453), channel_id=1, source_target_pairs={{0,2},{2,0},{4,6},{6,4},{8,10},{10,8},{12,14},{14,12},{1,3},{3,1},... | collective-permute-start | bytes 589832 | tf_op jit(solution)/shard_map/ppermute | solution.py:221
  5.5 1.6 %collective-permute-start.50 = (f32[6,16,512]{2,1,0:T(8,128)S(1)}, f32[6,16,512]{2,1,0:T(8,128)S(1)}, u32[]{:S(2)}, u32[]{:S(2)}) collective-permute-start(f32[6,16,512]{2,1,0:T(8,128)S(1)} %get-tuple-element.454), channel_id=1, source_target_pairs={{0,4},{2,6},{4,0},{6,2},{8,12},{10,14},{12,8},{14,10},{1,5},{3,7},... | collective-permute-start | bytes 589832 | tf_op jit(solution)/shard_map/ppermute | solution.py:221
  10.0 1.9 %collective-permute-start.48 = (s32[1]{0:T(128)}, s32[1]{0:T(128)}, u32[]{:S(2)}, u32[]{:S(2)}) collective-permute-start(s32[1]{0:T(128)} %bitcast.15), channel_id=1, source_target_pairs={{0,16},{16,0},{1,17},{17,1},{2,18},{18,2},{3,19},{19,3},{4,20},{20... | collective-permute-start | bytes 20 | tf_op jit(solution)/shard_map/ppermute | solution.py:306
  15.9 85.6 %conditional.1 = (f32[1,6,128,512]{3,2,1,0:T(8,128)S(1)}) conditional(s32[]{:T(128)} %bitcast.16, (s32[]{:T(128)}, s32[4]{0:T(128)S(1)}, s32[4]{0:T(128)S(1)}, s32[4]{0:T(128)S(1)}, s32[4]{0:T(128)S(1)}, /*index=5*/pred[4]{0:T(512)(128)(4,1)S(1)}, s32[4]{0:T(128)S(1)}, pred[4]{0:T(512)(128)(4,1)S(1)}, s32[]{:T(128)}, ...), branch_computations={%region_4.7_spmd, %region_7.10_spmd, %region_10.13_spmd} | conditional | flops 19661364 | bytes 28970012 | solution.py:353
  17.3 2.8 %collective-permute-start.14 = (f32[6,16,512]{2,1,0:T(8,128)S(1)}, f32[6,16,512]{2,1,0:T(8,128)S(1)}, u32[]{:S(2)}, u32[]{:S(2)}) collective-permute-start(f32[6,16,512]{2,1,0:T(8,128)S(1)} %get-tuple-element.379), channel_id=1, source_target_pairs={{0,8},{2,10},{4,12},{6,14},{8,0},{10,2},{12,4},{14,6},{1,9},{3,11}... | collective-permute-start | bytes 589832 | tf_op jit(solution)/shard_map/cond/branch_1_fun/ppermute | solution.py:221
  20.4 2.8 %collective-permute-start.16 = (f32[6,16,512]{2,1,0:T(8,128)S(1)}, f32[6,16,512]{2,1,0:T(8,128)S(1)}, u32[]{:S(2)}, u32[]{:S(2)}) collective-permute-start(f32[6,16,512]{2,1,0:T(8,128)S(1)} %get-tuple-element.381), channel_id=1, source_target_pairs={{0,8},{2,10},{4,12},{6,14},{8,0},{10,2},{12,4},{14,6},{1,9},{3,11}... | collective-permute-start | bytes 589832 | tf_op jit(solution)/shard_map/cond/branch_1_fun/ppermute | solution.py:221
  23.9 1.8 %branch_1_fun.9 = (f32[6,16,512]{2,1,0:T(8,128)S(1)}, f32[6,16,512]{2,1,0:T(8,128)S(1)}, f32[6,16,512]{2,1,0:T(8,128)S(1)}, f32[6,16,512]{2,1,0:T(8,128)S(1)}) custom-call(s32[4]{0:T(128)S(1)} %broadcast_add_fusion.1.starts_ref, f32[6,128,512]{2,1,0:T(8,128)} %get-tuple-element.386.block_ref, f32[6,16,512]{2,1,0:T(8,128)S(1)} %get-tuple-element.372.refs_1_.refs_0_, ...), custom_call_target="tpu_custom_call" | custom-call | bytes 1572864 | tf_op jit(solution)/shard_map/cond/branch_1_fun/pallas_call | solution.py:227
  25.7 1.6 %collective-permute-start.20 = (f32[6,16,512]{2,1,0:T(8,128)S(1)}, f32[6,16,512]{2,1,0:T(8,128)S(1)}, u32[]{:S(2)}, u32[]{:S(2)}) collective-permute-start(f32[6,16,512]{2,1,0:T(8,128)S(1)} %get-tuple-element.388), channel_id=1, source_target_pairs={{0,2},{2,0},{4,6},{6,4},{8,10},{10,8},{12,14},{14,12},{1,3},{3,1},... | collective-permute-start | bytes 589832 | tf_op jit(solution)/shard_map/cond/branch_1_fun/ppermute | solution.py:221
  27.3 1.6 %collective-permute-start.21 = (f32[6,16,512]{2,1,0:T(8,128)S(1)}, f32[6,16,512]{2,1,0:T(8,128)S(1)}, u32[]{:S(2)}, u32[]{:S(2)}) collective-permute-start(f32[6,16,512]{2,1,0:T(8,128)S(1)} %get-tuple-element.389), channel_id=1, source_target_pairs={{0,4},{2,6},{4,0},{6,2},{8,12},{10,14},{12,8},{14,10},{1,5},{3,7},... | collective-permute-start | bytes 589832 | tf_op jit(solution)/shard_map/cond/branch_1_fun/ppermute | solution.py:221
  28.9 9.3 %collective-permute-done.14.refs_4_ = f32[6,16,512]{2,1,0:T(8,128)S(1)} collective-permute-done((f32[6,16,512]{2,1,0:T(8,128)S(1)}, f32[6,16,512]{2,1,0:T(8,128)S(1)}, u32[]{:S(2)}, u32[]{:S(2)}) %collective-permute-start.14) | collective-permute-done | bytes 196640 | tf_op jit(solution)/shard_map/cond/branch_1_fun/ppermute | solution.py:221
  38.9 3.5 %collective-permute-done.15.refs_5_ = f32[6,16,512]{2,1,0:T(8,128)S(1)} collective-permute-done((f32[6,16,512]{2,1,0:T(8,128)S(1)}, f32[6,16,512]{2,1,0:T(8,128)S(1)}, u32[]{:S(2)}, u32[]{:S(2)}) %collective-permute-start.15) | collective-permute-done | bytes 196640 | tf_op jit(solution)/shard_map/cond/branch_1_fun/ppermute | solution.py:221
  42.5 3.1 %collective-permute-done.16.refs_6_ = f32[6,16,512]{2,1,0:T(8,128)S(1)} collective-permute-done((f32[6,16,512]{2,1,0:T(8,128)S(1)}, f32[6,16,512]{2,1,0:T(8,128)S(1)}, u32[]{:S(2)}, u32[]{:S(2)}) %collective-permute-start.16) | collective-permute-done | bytes 196640 | tf_op jit(solution)/shard_map/cond/branch_1_fun/ppermute | solution.py:221
  45.5 5.1 %collective-permute-done.22.refs_3_ = f32[6,16,512]{2,1,0:T(8,128)S(1)} collective-permute-done((f32[6,16,512]{2,1,0:T(8,128)S(1)}, f32[6,16,512]{2,1,0:T(8,128)S(1)}, u32[]{:S(2)}, u32[]{:S(2)}) %collective-permute-start.22) | collective-permute-done | bytes 196640 | tf_op jit(solution)/shard_map/cond/branch_1_fun/ppermute | solution.py:221
  52.0 2.3 %collective-permute-start.24 = (f32[6,16,512]{2,1,0:T(8,128)S(1)}, f32[6,16,512]{2,1,0:T(8,128)S(1)}, u32[]{:S(2)}, u32[]{:S(2)}) collective-permute-start(f32[6,16,512]{2,1,0:T(8,128)S(1)} %get-tuple-element.392), channel_id=1, source_target_pairs={{0,8},{2,10},{4,12},{6,14},{8,0},{10,2},{12,4},{14,6},{1,9},{3,11}... | collective-permute-start | bytes 589832 | tf_op jit(solution)/shard_map/cond/branch_1_fun/ppermute | solution.py:221
  56.3 1.6 %collective-permute-start.17 = (f32[6,16,512]{2,1,0:T(8,128)S(1)}, f32[6,16,512]{2,1,0:T(8,128)S(1)}, u32[]{:S(2)}, u32[]{:S(2)}) collective-permute-start(f32[6,16,512]{2,1,0:T(8,128)S(1)} %get-tuple-element.383), channel_id=1, source_target_pairs={{0,2},{2,0},{4,6},{6,4},{8,10},{10,8},{12,14},{14,12},{1,3},{3,1},... | collective-permute-start | bytes 589832 | tf_op jit(solution)/shard_map/cond/branch_1_fun/ppermute | solution.py:221
  57.9 2.5 %collective-permute-start.18 = (f32[6,16,512]{2,1,0:T(8,128)S(1)}, f32[6,16,512]{2,1,0:T(8,128)S(1)}, u32[]{:S(2)}, u32[]{:S(2)}) collective-permute-start(f32[6,16,512]{2,1,0:T(8,128)S(1)} %get-tuple-element.384), channel_id=1, source_target_pairs={{0,4},{2,6},{4,0},{6,2},{8,12},{10,14},{12,8},{14,10},{1,5},{3,7},... | collective-permute-start | bytes 589832 | tf_op jit(solution)/shard_map/cond/branch_1_fun/ppermute | solution.py:221
  60.3 12.3 %collective-permute-done.23.refs_4_ = f32[6,16,512]{2,1,0:T(8,128)S(1)} collective-permute-done((f32[6,16,512]{2,1,0:T(8,128)S(1)}, f32[6,16,512]{2,1,0:T(8,128)S(1)}, u32[]{:S(2)}, u32[]{:S(2)}) %collective-permute-start.23) | collective-permute-done | bytes 196640 | tf_op jit(solution)/shard_map/cond/branch_1_fun/ppermute | solution.py:221
  73.7 3.3 %collective-permute-done.24.refs_5_ = f32[6,16,512]{2,1,0:T(8,128)S(1)} collective-permute-done((f32[6,16,512]{2,1,0:T(8,128)S(1)}, f32[6,16,512]{2,1,0:T(8,128)S(1)}, u32[]{:S(2)}, u32[]{:S(2)}) %collective-permute-start.24) | collective-permute-done | bytes 196640 | tf_op jit(solution)/shard_map/cond/branch_1_fun/ppermute | solution.py:221
  77.0 3.3 %collective-permute-done.25.refs_6_ = f32[6,16,512]{2,1,0:T(8,128)S(1)} collective-permute-done((f32[6,16,512]{2,1,0:T(8,128)S(1)}, f32[6,16,512]{2,1,0:T(8,128)S(1)}, u32[]{:S(2)}, u32[]{:S(2)}) %collective-permute-start.25) | collective-permute-done | bytes 196640 | tf_op jit(solution)/shard_map/cond/branch_1_fun/ppermute | solution.py:221
  81.6 3.0 %collective-permute-start.28 = (f32[6,16,512]{2,1,0:T(8,128)S(1)}, f32[6,16,512]{2,1,0:T(8,128)S(1)}, u32[]{:S(2)}, u32[]{:S(2)}) collective-permute-start(f32[6,16,512]{2,1,0:T(8,128)S(1)} %get-tuple-element.397), channel_id=1, source_target_pairs={{0,6},{2,4},{4,2},{6,0},{8,14},{10,12},{12,10},{14,8},{1,7},{3,5},... | collective-permute-start | bytes 589832 | tf_op jit(solution)/shard_map/cond/branch_1_fun/ppermute | solution.py:221
  86.7 3.7 %collective-permute-done.26.refs_5_ = f32[6,16,512]{2,1,0:T(8,128)S(1)} collective-permute-done((f32[6,16,512]{2,1,0:T(8,128)S(1)}, f32[6,16,512]{2,1,0:T(8,128)S(1)}, u32[]{:S(2)}, u32[]{:S(2)}) %collective-permute-start.26) | collective-permute-done | bytes 196640 | tf_op jit(solution)/shard_map/cond/branch_1_fun/ppermute | solution.py:221
  90.4 2.3 %collective-permute-done.28.refs_7_ = f32[6,16,512]{2,1,0:T(8,128)S(1)} collective-permute-done((f32[6,16,512]{2,1,0:T(8,128)S(1)}, f32[6,16,512]{2,1,0:T(8,128)S(1)}, u32[]{:S(2)}, u32[]{:S(2)}) %collective-permute-start.28) | collective-permute-done | bytes 196640 | tf_op jit(solution)/shard_map/cond/branch_1_fun/ppermute | solution.py:221
  92.7 8.8 %branch_1_fun.13 = f32[6,128,512]{2,1,0:T(8,128)S(1)} custom-call(s32[1]{0:T(128)} %bitcast.5.place_ref, s32[8]{0:T(128)S(1)} %pad_add_fusion.2.starts_ref, f32[6,16,512]{2,1,0:T(8,128)S(1)} %get-tuple-element.382.refs_0_, f32[6,16,512]{2,1,0:T(8,128)S(1)} %collective-permute-done.17.refs_1_, f32[6,16,512]{2,1,0:T(8,128)S(1)} %collective-permute-done.18.refs_2_, ...), custom_call_target="tpu_custom_call" | custom-call | flops 19660800 | bytes 3407872 | tf_op jit(solution)/shard_map/cond/branch_1_fun/pallas_call | solution.py:175
  (96 shorter events, 16.6 us)
Async XLA Ops:
  2.5 12.6 %collective-permute-start.49 = (f32[6,16,512]{2,1,0:T(8,128)S(1)}, f32[6,16,512]{2,1,0:T(8,128)S(1)}, u32[]{:S(2)}, u32[]{:S(2)}) collective-permute-start(f32[6,16,512]{2,1,0:T(8,128)S(1)} %get-tuple-element.453), channel_id=1, source_target_pairs={{0,2},{2,0},{4,6},{6,4},{8,10},{10,8},{12,14},{14,12},{1,3},{3,1},... | collective-permute-start | bytes 589832 | tf_op jit(solution)/shard_map/ppermute | solution.py:221
  5.5 9.6 %collective-permute-start.50 = (f32[6,16,512]{2,1,0:T(8,128)S(1)}, f32[6,16,512]{2,1,0:T(8,128)S(1)}, u32[]{:S(2)}, u32[]{:S(2)}) collective-permute-start(f32[6,16,512]{2,1,0:T(8,128)S(1)} %get-tuple-element.454), channel_id=1, source_target_pairs={{0,4},{2,6},{4,0},{6,2},{8,12},{10,14},{12,8},{14,10},{1,5},{3,7},... | collective-permute-start | bytes 589832 | tf_op jit(solution)/shard_map/ppermute | solution.py:221
  7.1 8.8 %collective-permute-start.51 = (f32[6,16,512]{2,1,0:T(8,128)S(1)}, f32[6,16,512]{2,1,0:T(8,128)S(1)}, u32[]{:S(2)}, u32[]{:S(2)}) collective-permute-start(f32[6,16,512]{2,1,0:T(8,128)S(1)} %get-tuple-element.455), channel_id=1, source_target_pairs={{0,6},{2,4},{4,2},{6,0},{8,14},{10,12},{12,10},{14,8},{1,7},{3,5},... | collective-permute-start | bytes 589832 | tf_op jit(solution)/shard_map/ppermute | solution.py:221
  8.5 6.6 %collective-permute-start.52 = (f32[8,512]{1,0:T(8,128)S(1)}, f32[8,512]{1,0:T(8,128)S(1)}, u32[]{:S(2)}, u32[]{:S(2)}) collective-permute-start(f32[8,512]{1,0:T(8,128)S(1)} %dynamic-slice_bitcast_fusion.3), channel_id=1, source_target_pairs={{0,1},{1,0},{2,3},{3,2},{4,5},{5,4},{6,7},{7,6},{8,9},{9,8},{10,11... | collective-permute-start | bytes 49160 | tf_op jit(solution)/shard_map/ppermute | solution.py:201
  10.0 3.7 %collective-permute-start.48 = (s32[1]{0:T(128)}, s32[1]{0:T(128)}, u32[]{:S(2)}, u32[]{:S(2)}) collective-permute-start(s32[1]{0:T(128)} %bitcast.15), channel_id=1, source_target_pairs={{0,16},{16,0},{1,17},{17,1},{2,18},{18,2},{3,19},{19,3},{4,20},{20... | collective-permute-start | bytes 20 | tf_op jit(solution)/shard_map/ppermute | solution.py:306
  16.0 35.3 %copy-start.1 = (f32[6,16,512]{2,1,0:T(8,128)}, f32[6,16,512]{2,1,0:T(8,128)S(1)}, u32[]{:S(2)}) copy-start(f32[6,16,512]{2,1,0:T(8,128)S(1)} %get-tuple-element.373.refs_2_.refs_1_) | copy-start | bytes 589828 | tf_op jit(solution)/shard_map/cond
  17.3 20.9 %collective-permute-start.14 = (f32[6,16,512]{2,1,0:T(8,128)S(1)}, f32[6,16,512]{2,1,0:T(8,128)S(1)}, u32[]{:S(2)}, u32[]{:S(2)}) collective-permute-start(f32[6,16,512]{2,1,0:T(8,128)S(1)} %get-tuple-element.379), channel_id=1, source_target_pairs={{0,8},{2,10},{4,12},{6,14},{8,0},{10,2},{12,4},{14,6},{1,9},{3,11}... | collective-permute-start | bytes 589832 | tf_op jit(solution)/shard_map/cond/branch_1_fun/ppermute | solution.py:221
  20.1 22.4 %collective-permute-start.15 = (f32[6,16,512]{2,1,0:T(8,128)S(1)}, f32[6,16,512]{2,1,0:T(8,128)S(1)}, u32[]{:S(2)}, u32[]{:S(2)}) collective-permute-start(f32[6,16,512]{2,1,0:T(8,128)S(1)} %get-tuple-element.380), channel_id=1, source_target_pairs={{0,8},{2,10},{4,12},{6,14},{8,0},{10,2},{12,4},{14,6},{1,9},{3,11}... | collective-permute-start | bytes 589832 | tf_op jit(solution)/shard_map/cond/branch_1_fun/ppermute | solution.py:221
  20.4 25.2 %collective-permute-start.16 = (f32[6,16,512]{2,1,0:T(8,128)S(1)}, f32[6,16,512]{2,1,0:T(8,128)S(1)}, u32[]{:S(2)}, u32[]{:S(2)}) collective-permute-start(f32[6,16,512]{2,1,0:T(8,128)S(1)} %get-tuple-element.381), channel_id=1, source_target_pairs={{0,8},{2,10},{4,12},{6,14},{8,0},{10,2},{12,4},{14,6},{1,9},{3,11}... | collective-permute-start | bytes 589832 | tf_op jit(solution)/shard_map/cond/branch_1_fun/ppermute | solution.py:221
  23.2 31.8 %copy-start.4 = (f32[6,16,512]{2,1,0:T(8,128)S(1)}, f32[6,16,512]{2,1,0:T(8,128)}, u32[]{:S(2)}) copy-start(f32[6,16,512]{2,1,0:T(8,128)} %copy-done.3) | copy-start | bytes 589828 | tf_op jit(solution)/shard_map/cond
  25.7 19.8 %collective-permute-start.20 = (f32[6,16,512]{2,1,0:T(8,128)S(1)}, f32[6,16,512]{2,1,0:T(8,128)S(1)}, u32[]{:S(2)}, u32[]{:S(2)}) collective-permute-start(f32[6,16,512]{2,1,0:T(8,128)S(1)} %get-tuple-element.388), channel_id=1, source_target_pairs={{0,2},{2,0},{4,6},{6,4},{8,10},{10,8},{12,14},{14,12},{1,3},{3,1},... | collective-permute-start | bytes 589832 | tf_op jit(solution)/shard_map/cond/branch_1_fun/ppermute | solution.py:221
  27.3 18.2 %collective-permute-start.21 = (f32[6,16,512]{2,1,0:T(8,128)S(1)}, f32[6,16,512]{2,1,0:T(8,128)S(1)}, u32[]{:S(2)}, u32[]{:S(2)}) collective-permute-start(f32[6,16,512]{2,1,0:T(8,128)S(1)} %get-tuple-element.389), channel_id=1, source_target_pairs={{0,4},{2,6},{4,0},{6,2},{8,12},{10,14},{12,8},{14,10},{1,5},{3,7},... | collective-permute-start | bytes 589832 | tf_op jit(solution)/shard_map/cond/branch_1_fun/ppermute | solution.py:221
  38.2 12.5 %collective-permute-start.22 = (f32[6,16,512]{2,1,0:T(8,128)S(1)}, f32[6,16,512]{2,1,0:T(8,128)S(1)}, u32[]{:S(2)}, u32[]{:S(2)}) collective-permute-start(f32[6,16,512]{2,1,0:T(8,128)S(1)} %get-tuple-element.390), channel_id=1, source_target_pairs={{0,6},{2,4},{4,2},{6,0},{8,14},{10,12},{12,10},{14,8},{1,7},{3,5},... | collective-permute-start | bytes 589832 | tf_op jit(solution)/shard_map/cond/branch_1_fun/ppermute | solution.py:221
  51.3 21.4 %collective-permute-start.23 = (f32[6,16,512]{2,1,0:T(8,128)S(1)}, f32[6,16,512]{2,1,0:T(8,128)S(1)}, u32[]{:S(2)}, u32[]{:S(2)}) collective-permute-start(f32[6,16,512]{2,1,0:T(8,128)S(1)} %get-tuple-element.391), channel_id=1, source_target_pairs={{0,8},{2,10},{4,12},{6,14},{8,0},{10,2},{12,4},{14,6},{1,9},{3,11}... | collective-permute-start | bytes 589832 | tf_op jit(solution)/shard_map/cond/branch_1_fun/ppermute | solution.py:221
  52.0 25.0 %collective-permute-start.24 = (f32[6,16,512]{2,1,0:T(8,128)S(1)}, f32[6,16,512]{2,1,0:T(8,128)S(1)}, u32[]{:S(2)}, u32[]{:S(2)}) collective-permute-start(f32[6,16,512]{2,1,0:T(8,128)S(1)} %get-tuple-element.392), channel_id=1, source_target_pairs={{0,8},{2,10},{4,12},{6,14},{8,0},{10,2},{12,4},{14,6},{1,9},{3,11}... | collective-permute-start | bytes 589832 | tf_op jit(solution)/shard_map/cond/branch_1_fun/ppermute | solution.py:221
  54.3 26.0 %collective-permute-start.25 = (f32[6,16,512]{2,1,0:T(8,128)S(1)}, f32[6,16,512]{2,1,0:T(8,128)S(1)}, u32[]{:S(2)}, u32[]{:S(2)}) collective-permute-start(f32[6,16,512]{2,1,0:T(8,128)S(1)} %get-tuple-element.393), channel_id=1, source_target_pairs={{0,8},{2,10},{4,12},{6,14},{8,0},{10,2},{12,4},{14,6},{1,9},{3,11}... | collective-permute-start | bytes 589832 | tf_op jit(solution)/shard_map/cond/branch_1_fun/ppermute | solution.py:221
  56.3 36.4 %copy-start.9 = (f32[8,512]{1,0:T(8,128)S(1)}, f32[8,512]{1,0:T(8,128)}, u32[]{:S(2)}) copy-start(f32[8,512]{1,0:T(8,128)} %copy-done.8) | copy-start | bytes 49156 | tf_op jit(solution)/shard_map/cond
  56.3 25.3 %collective-permute-start.17 = (f32[6,16,512]{2,1,0:T(8,128)S(1)}, f32[6,16,512]{2,1,0:T(8,128)S(1)}, u32[]{:S(2)}, u32[]{:S(2)}) collective-permute-start(f32[6,16,512]{2,1,0:T(8,128)S(1)} %get-tuple-element.383), channel_id=1, source_target_pairs={{0,2},{2,0},{4,6},{6,4},{8,10},{10,8},{12,14},{14,12},{1,3},{3,1},... | collective-permute-start | bytes 589832 | tf_op jit(solution)/shard_map/cond/branch_1_fun/ppermute | solution.py:221
  57.9 26.8 %collective-permute-start.18 = (f32[6,16,512]{2,1,0:T(8,128)S(1)}, f32[6,16,512]{2,1,0:T(8,128)S(1)}, u32[]{:S(2)}, u32[]{:S(2)}) collective-permute-start(f32[6,16,512]{2,1,0:T(8,128)S(1)} %get-tuple-element.384), channel_id=1, source_target_pairs={{0,4},{2,6},{4,0},{6,2},{8,12},{10,14},{12,8},{14,10},{1,5},{3,7},... | collective-permute-start | bytes 589832 | tf_op jit(solution)/shard_map/cond/branch_1_fun/ppermute | solution.py:221
  72.7 12.0 %collective-permute-start.19 = (f32[6,16,512]{2,1,0:T(8,128)S(1)}, f32[6,16,512]{2,1,0:T(8,128)S(1)}, u32[]{:S(2)}, u32[]{:S(2)}) collective-permute-start(f32[6,16,512]{2,1,0:T(8,128)S(1)} %get-tuple-element.385), channel_id=1, source_target_pairs={{0,6},{2,4},{4,2},{6,0},{8,14},{10,12},{12,10},{14,8},{1,7},{3,5},... | collective-permute-start | bytes 589832 | tf_op jit(solution)/shard_map/cond/branch_1_fun/ppermute | solution.py:221
  81.1 9.3 %collective-permute-start.26 = (f32[6,16,512]{2,1,0:T(8,128)S(1)}, f32[6,16,512]{2,1,0:T(8,128)S(1)}, u32[]{:S(2)}, u32[]{:S(2)}) collective-permute-start(f32[6,16,512]{2,1,0:T(8,128)S(1)} %get-tuple-element.395), channel_id=1, source_target_pairs={{0,2},{2,0},{4,6},{6,4},{8,10},{10,8},{12,14},{14,12},{1,3},{3,1},... | collective-permute-start | bytes 589832 | tf_op jit(solution)/shard_map/cond/branch_1_fun/ppermute | solution.py:221
  81.6 8.8 %collective-permute-start.27 = (f32[6,16,512]{2,1,0:T(8,128)S(1)}, f32[6,16,512]{2,1,0:T(8,128)S(1)}, u32[]{:S(2)}, u32[]{:S(2)}) collective-permute-start(f32[6,16,512]{2,1,0:T(8,128)S(1)} %get-tuple-element.396), channel_id=1, source_target_pairs={{0,4},{2,6},{4,0},{6,2},{8,12},{10,14},{12,8},{14,10},{1,5},{3,7},... | collective-permute-start | bytes 589832 | tf_op jit(solution)/shard_map/cond/branch_1_fun/ppermute | solution.py:221
  81.6 11.1 %collective-permute-start.28 = (f32[6,16,512]{2,1,0:T(8,128)S(1)}, f32[6,16,512]{2,1,0:T(8,128)S(1)}, u32[]{:S(2)}, u32[]{:S(2)}) collective-permute-start(f32[6,16,512]{2,1,0:T(8,128)S(1)} %get-tuple-element.397), channel_id=1, source_target_pairs={{0,6},{2,4},{4,2},{6,0},{8,14},{10,12},{12,10},{14,8},{1,7},{3,5},... | collective-permute-start | bytes 589832 | tf_op jit(solution)/shard_map/cond/branch_1_fun/ppermute | solution.py:221
  85.3 1.4 %collective-permute-start.29 = (f32[6,8,512]{2,1,0:T(8,128)S(1)}, f32[6,8,512]{2,1,0:T(8,128)S(1)}, u32[]{:S(2)}, u32[]{:S(2)}) collective-permute-start(f32[6,8,512]{2,1,0:T(8,128)S(1)} %branch_1_fun.12), channel_id=1, source_target_pairs={{0,1},{1,0},{2,3},{3,2},{4,5},{5,4},{6,7},{7,6},{8,9},{9,8},{10,11... | collective-permute-start | bytes 294920 | tf_op jit(solution)/shard_map/cond/branch_1_fun/ppermute | solution.py:201
  (19 other events, 270.2 us)

commit v2 on v1

--- a/solution.py
+++ b/solution.py
@@ -17,19 +17,20 @@
 
 TILE = 8
 LANES = 128
+SLABS = 4
 
 
 HEIGHT_SCALE = TIME_STEP * TIME_STEP / 2
 SPEED_SCALE = TIME_STEP / 2
 
 
-def stencil_kernel(count, pieces, place_ref, starts_ref, *refs):
+def stencil_kernel(count, chunks, pieces, here_ref, *refs):
     parent_refs = refs[:pieces]
-    low_ref, high_ref, force_ref, force_low_ref, force_high_ref, out_ref, first, second, force = refs[pieces:]
+    low_ref, high_ref, force_ref, force_low_ref, force_high_ref, out_ref, first, second, force, result, sem = refs[pieces:]
     rows, columns = force_ref.shape
     blocks = rows // TILE
     strips = columns // LANES
-    place = place_ref[0]
+    place = here_ref[1]
     total = float(rows * count)
     tile = (TILE, LANES)
     sub = lax.broadcasted_iota(jnp.int32, tile, 0)
@@ -57,8 +58,9 @@
                 buffer[field, strip, last : last + TILE] = high
             for piece, parent_ref in enumerate(parent_refs):
                 height = parent_ref.shape[1]
-                here = pl.ds(pl.multiple_of(head + starts_ref[piece], TILE), height)
-                first[field, strip, here] = scaled(field, parent_ref[field, :, span])
+                first_row = head if pieces == 1 else head + part_start(here_ref, chunks[piece // PARTS], piece % PARTS, rows)
+                span_rows = pl.ds(pl.multiple_of(first_row, TILE), height)
+                first[field, strip, span_rows] = scaled(field, parent_ref[field, :, span])
             if field % 3 == 2:
                 edge = first[field, strip, head : head + TILE]
                 first[field, strip, head : head + TILE] = jnp.where(sub + place > 0, edge, 0.0)
@@ -87,7 +89,7 @@
     def give(field, block, values):
         for strip in range(strips):
             value = values[strip] * (1.0 / HEIGHT_SCALE) - 1.0 if field % 3 == 0 else values[strip] * (1.0 / SPEED_SCALE)
-            out_ref[field, pl.ds(pl.multiple_of(TILE * (block - 1), TILE), TILE), strip * LANES : (strip + 1) * LANES] = value
+            result[field, pl.ds(pl.multiple_of(TILE * (block - 1), TILE), TILE), strip * LANES : (strip + 1) * LANES] = value
 
     def heights(source, target, block):
         for base in (0, 3):
@@ -155,32 +157,47 @@
         speeds(source, target, block, give)
         return carry
 
-    lax.fori_loop(1, blocks + 1, finish, 0)
-
-    @pl.when(place == 0)
-    def _():
-        for field in (2, 5):
-            for strip in range(strips):
-                span = slice(strip * LANES, (strip + 1) * LANES)
-                out_ref[field, :TILE, span] = jnp.where(bottom, 0.0, out_ref[field, :TILE, span])
-
-
-def stencil(parents, starts, edges, forcing, force_edges):
+    copies = []
+    for part in range(SLABS):
+        first_block, end_block = part * blocks // SLABS, (part + 1) * blocks // SLABS
+        lax.fori_loop(first_block + 1, end_block + 1, finish, 0)
+        if part == 0:
+
+            @pl.when(place == 0)
+            def _():
+                for field in (2, 5):
+                    for strip in range(strips):
+                        span = slice(strip * LANES, (strip + 1) * LANES)
+                        result[field, :TILE, span] = jnp.where(bottom, 0.0, result[field, :TILE, span])
+
+        slab = slice(TILE * first_block, TILE * end_block)
+        copies.append(pltpu.make_async_copy(result.at[:, slab, :], out_ref.at[:, slab, :], sem.at[part]))
+        copies[-1].start()
+    for copy in copies:
+        copy.wait()
+
+
+def stencil(here, parents, edges, forcing, force_edges):
     rows, columns = forcing.shape
     fields_count = parents[0].shape[0]
     shape = (fields_count, columns // LANES, rows + 5 * TILE, LANES)
     vmem = pl.BlockSpec(memory_space=pltpu.VMEM)
     smem = pl.BlockSpec(memory_space=pltpu.SMEM)
-    place = lax.axis_index("lat").astype(jnp.int32)[None]
     return pl.pallas_call(
-        functools.partial(stencil_kernel, lax.axis_size("lat"), len(parents)),
+        functools.partial(stencil_kernel, lax.axis_size("lat"), chunks_of(rows), len(parents)),
         out_shape=jax.ShapeDtypeStruct((fields_count, rows, columns), jnp.float32),
-        in_specs=[smem] * 2 + [vmem] * (len(parents) + 5),
-        out_specs=vmem,
-        scratch_shapes=[pltpu.VMEM(shape, jnp.float32), pltpu.VMEM(shape, jnp.float32), pltpu.VMEM(shape[1:], jnp.float32)],
+        in_specs=[smem] + [vmem] * (len(parents) + 5),
+        out_specs=pl.BlockSpec(memory_space=pltpu.HBM),
+        scratch_shapes=[
+            pltpu.VMEM(shape, jnp.float32),
+            pltpu.VMEM(shape, jnp.float32),
+            pltpu.VMEM(shape[1:], jnp.float32),
+            pltpu.VMEM((fields_count, rows, columns), jnp.float32),
+            pltpu.SemaphoreType.DMA((SLABS,)),
+        ],
         compiler_params=pltpu.CompilerParams(vmem_limit_bytes=12 << 20),
         cost_estimate=pl.CostEstimate(flops=300 * rows * columns, bytes_accessed=52 * rows * columns, transcendentals=0),
-    )(place, starts, *parents, *edges, forcing, *force_edges)
+    )(here, *parents, *edges, forcing, *force_edges)
 
 
 def edge_rows(block):
@@ -214,33 +231,50 @@
 
 PARTS = 4
 MEMBERS = 2 * PARTS
-CHUNKS = 2
+CHUNKS = (1, 1)
+
+
+def chunks_of(rows):
+    spans = [rows * share // sum(CHUNKS) for share in CHUNKS]
+    return [(sum(spans[:c]), span) for c, span in enumerate(spans)]
+
+
+def part_start(here_ref, chunk, k, rows):
+    passed, span = chunk
+    own = lax.rem(here_ref[0], PARTS)
+    return jnp.where(here_ref[1] == 0, rows - passed - span, passed) + (own ^ k) * (span // PARTS)
 
 
 def shift(values, distance):
     return lax.ppermute(values, "mem", [(i, i ^ distance) for i in range(MEMBERS)])
 
 
-def small_call(kernel, count, shape, scalars, arrays, held, scratch=()):
+def small_call(kernel, outs, here, tables, arrays, left, scratch=()):
     vmem = pl.BlockSpec(memory_space=pltpu.VMEM)
-    size = 4 * shape[0] * shape[1] * shape[2]
+    smem = pl.BlockSpec(memory_space=pltpu.SMEM)
+    anywhere = pl.BlockSpec(memory_space=pl.ANY)
+    moved = sum(2 * out.size * 4 for out in outs)
     return pl.pallas_call(
         kernel,
-        out_shape=[jax.ShapeDtypeStruct(shape, jnp.float32)] * count,
-        in_specs=[pl.BlockSpec(memory_space=pltpu.SMEM)] + [vmem] * held + [pl.BlockSpec(memory_space=pl.ANY)] * (len(arrays) - held),
-        out_specs=[vmem] * count,
+        out_shape=outs,
+        in_specs=[smem] * (1 + len(tables)) + [vmem] * len(arrays) + [anywhere] * len(left),
+        out_specs=[vmem if out.ndim > 1 else smem for out in outs],
         scratch_shapes=list(scratch),
         compiler_params=pltpu.CompilerParams(vmem_limit_bytes=4 << 20),
-        cost_estimate=pl.CostEstimate(flops=0, bytes_accessed=2 * count * size, transcendentals=0),
-    )(scalars, *arrays)
-
-
-def cut_kernel(starts_ref, block_ref, *refs):
-    outs, sem = refs[-PARTS - 1 : -1], refs[-1]
-    height = outs[0].shape[1]
+        cost_estimate=pl.CostEstimate(flops=0, bytes_accessed=moved, transcendentals=0),
+    )(here, *tables, *arrays, *left)
+
+
+def part_shape(block, chunk):
+    return jax.ShapeDtypeStruct((block.shape[0], chunk[1] // PARTS, block.shape[2]), jnp.float32)
+
+
+def cut_kernel(chunk, here_ref, block_ref, *refs):
+    outs, sem = refs[-PARTS:-1], refs[-1]
     copies = []
     for k, out in enumerate(outs):
-        rows = pl.ds(pl.multiple_of(starts_ref[k], TILE), height)
+        first_row = part_start(here_ref, chunk, k + 1, block_ref.shape[1])
+        rows = pl.ds(pl.multiple_of(first_row, TILE), out.shape[1])
         copies.append(pltpu.make_async_copy(block_ref.at[:, rows, :], out, sem.at[k]))
     for copy in copies:
         copy.start()
@@ -248,110 +282,129 @@
         copy.wait()
 
 
-def cut(block, starts, height, after):
-    shape = (block.shape[0], height, block.shape[2])
-    return small_call(cut_kernel, PARTS, shape, starts, [block, *after], 0, [pltpu.SemaphoreType.DMA((PARTS,))])
-
-
-def route_kernel(sources, count, chosen_ref, *refs):
-    for k, out in enumerate(refs[-count:]):
-        for j, source in enumerate(refs[:sources]):
-
-            @pl.when(chosen_ref[k] == j)
+def cut(here, block, chunk, after):
+    outs = [part_shape(block, chunk)] * (PARTS - 1)
+    kernel = functools.partial(cut_kernel, chunk)
+    return small_call(kernel, outs, here, [], [], [block, *after], [pltpu.SemaphoreType.DMA((PARTS - 1,))])
+
+
+def route_kernel(chunk, sources, count, here_ref, chosen_ref, *refs):
+    source_refs, block_ref = refs[:sources], refs[sources]
+    outs, sem = refs[-count - 1 : -1], refs[-1]
+    first_row = part_start(here_ref, chunk, 0, block_ref.shape[1])
+    rows = pl.ds(pl.multiple_of(first_row, TILE), outs[0].shape[1])
+    copies = [pltpu.make_async_copy(block_ref.at[:, rows, :], out, sem.at[k]) for k, out in enumerate(outs)]
+    for k, copy in enumerate(copies):
+        pl.when(chosen_ref[k] == 0)(copy.start)
+    for k, out in enumerate(outs):
+        for j, source in enumerate(source_refs):
+
+            @pl.when(chosen_ref[k] == j + 1)
             def _():
                 out[...] = source[...]
 
-
-def route(chosen, sources, count, after=()):
-    kernel = functools.partial(route_kernel, len(sources), count)
-    return small_call(kernel, count, sources[0].shape, chosen, [*sources, *after], len(sources))
-
-
-def edge_kernel(chosen_ref, *refs):
+    for k, copy in enumerate(copies):
+        pl.when(chosen_ref[k] == 0)(copy.wait)
+
+
+def route(here, chosen, count, block, chunk, sources, after=()):
+    outs = [part_shape(block, chunk)] * count
+    kernel = functools.partial(route_kernel, chunk, len(sources), count)
+    return small_call(kernel, outs, here, [chosen], sources, [block, *after], [pltpu.SemaphoreType.DMA((count,))])
+
+
+def edge_kernel(here_ref, *refs):
     out = refs[-1]
-    for j, source in enumerate(refs[:-1]):
-
-        @pl.when(chosen_ref[0] == j)
-        def _():
-            out[...] = source[:, pl.ds(pl.multiple_of(chosen_ref[1], TILE), TILE), :]
-
-
-def crossings(ancestors):
-    ids = jnp.arange(MEMBERS, dtype=jnp.int32)
-    far = ids[:, None] // PARTS != ids[None, :] // PARTS
-    need = jnp.any((ancestors[:, None] == ids[None, :]) & far, axis=0)
-    ahead = need[:, None] & (ids[:, None] < ids[None, :]) & ~far
-    return need, jnp.sum(ahead.astype(jnp.int32), axis=0)
-
-
-def by_crossings(block, ancestors, finish):
-    fields_count, rows, columns = block.shape
-    ids = jnp.arange(MEMBERS, dtype=jnp.int32)
-    member = lax.axis_index("mem").astype(jnp.int32)
-    half, own = member // PARTS, member % PARTS
-    parts = own ^ jnp.arange(PARTS, dtype=jnp.int32)
-    span = rows // CHUNKS
-    height = span // PARTS
-    near = (lax.axis_index("lat") == 0).astype(jnp.int32)
-    starts = [((CHUNKS - 1 - c) * near + c * (1 - near)) * span + parts * height for c in range(CHUNKS)]
-
-    def spread(c, block, after):
-        held = cut(block, starts[c], height, after)
-        return [held[0]] + [shift(held[k], k) for k in range(1, PARTS)]
-
-    need, rank = crossings(ancestors)
-    most = jnp.max(rank + need.astype(jnp.int32))[None]
+    own = lax.rem(here_ref[0], PARTS)
+    rows = refs[0].shape[1]
+    for k, source in enumerate(refs[:PARTS]):
+        for place, owner, first_row in ((0, PARTS - 1, rows - TILE), (1, 0, 0)):
+
+            @pl.when((here_ref[1] == place) & ((own ^ k) == owner))
+            def _():
+                out[...] = source[:, first_row : first_row + TILE, :]
+
+
+def tables_kernel(here_ref, ancestors_ref, *refs):
+    order_ref, given_ref, most_ref, rank_ref = refs[-4:]
+    member = here_ref[0]
+    half, own = member // PARTS, lax.rem(member, PARTS)
+    for r in range(PARTS):
+        order_ref[r] = 0
+    most = 0
+    for side in range(2):
+        rank = 0
+        for place in range(PARTS):
+            p = side * PARTS + place
+            need = 0
+            for slot in range((1 - side) * PARTS, (2 - side) * PARTS):
+                need = need | jnp.where(ancestors_ref[slot] == p, 1, 0)
+            rank_ref[p] = rank
+
+            @pl.when((need > 0) & (half == side))
+            def _():
+                order_ref[rank] = own ^ place
+
+            rank = rank + need
+        most = jnp.maximum(most, rank)
+    most_ref[0] = most
+    for k in range(PARTS):
+        parent = ancestors_ref[half * PARTS + (own ^ k)]
+        given_ref[k] = jnp.where(parent // PARTS == half, lax.rem(parent, PARTS) ^ own, PARTS + rank_ref[parent])
+
+
+def tables_of(here, ancestors, after):
+    outs = [jax.ShapeDtypeStruct((size,), jnp.int32) for size in (PARTS, PARTS, 1)]
+    return small_call(tables_kernel, outs, here, [ancestors], [], after, [pltpu.SMEM((MEMBERS,), jnp.int32)])
+
+
+def by_crossings(here, block, ancestors):
+    chunks = chunks_of(block.shape[1])
+
+    def spread(held):
+        return [shift(part, k + 1) for k, part in enumerate(held)]
+
+    held = cut(here, block, chunks[0], ())
+    shared = spread(held)
+    order, given_index, most = tables_of(here, ancestors, held[:1])
     groups = lax.axis_size("groups")
-    for distance in range(1, groups):
-        other = lax.ppermute(most, "groups", [(i, (i + distance) % groups) for i in range(groups)])
+    other = most
+    for _ in range(groups - 1):
+        other = lax.ppermute(other, "groups", [(i, (i + 1) % groups) for i in range(groups)])
         most = jnp.maximum(most, other)
-    slots = half * PARTS + parts
-    parent = jnp.sum(jnp.where(slots[:, None] == ids[None, :], ancestors[None, :], 0), axis=1)
-    parent_rank = jnp.sum(jnp.where(parent[:, None] == ids[None, :], rank[None, :], 0), axis=1)
-    given_index = jnp.where(parent // PARTS == half, (parent % PARTS) ^ own, PARTS + parent_rank)
-
-    def plan(rounds, block, shared, need, rank, given_index, rest):
-        turns = jnp.arange(rounds, dtype=jnp.int32)
-        mine = need & (ids // PARTS == half)
-        order = jnp.sum(jnp.where(mine[None, :] & (rank[None, :] == turns[:, None]), ids[None, :] % PARTS, 0), axis=1)
+
+    def plan(rounds, here, block, shared, order, given_index):
         crossed, final = (), []
-        for c in range(CHUNKS):
-            if c > 0:
-                shared = spread(c, block, shared[1:])
-            sent = route(order ^ own, shared, rounds, crossed)
+        for c, chunk in enumerate(chunks):
+            sent = route(here, order, rounds, block, chunk, shared, crossed[:1])
+            following = ()
+            if c + 1 < len(chunks):
+                following = spread(cut(here, block, chunks[c + 1], (*shared, sent[0])))
             crossed = [shift(part, PARTS) for part in sent]
-            given = route(given_index, [*shared, *crossed], PARTS)
+            given = route(here, given_index, PARTS, block, chunk, [*shared, *crossed])
             final.append([given[0]] + [shift(given[k], k) for k in range(1, PARTS)])
-        return finish(final, starts, *rest)
-
-    return spread(0, block, ()), most, (need, rank, given_index), plan
+            shared = following
+        edge_shape = jax.ShapeDtypeStruct((block.shape[0], TILE, block.shape[2]), jnp.float32)
+        edge = small_call(edge_kernel, [edge_shape], here, [], final[0], [])[0]
+        return [part for parts in final for part in parts], swap_edges(edge)[0]
+
+    branches = [functools.partial(plan, rounds) for rounds in range(2, PARTS + 1)]
+    return lax.switch(jnp.clip(most[0] - 2, 0, PARTS - 2), branches, here, block, shared, order, given_index)
 
 
 def on_device(ensemble, forcing_table, ancestors, selector):
     rows = ensemble.shape[2]
     block = ensemble.reshape(ensemble.shape[1:])
+    here = jnp.stack([lax.axis_index("mem"), lax.axis_index("lat")]).astype(jnp.int32)
     forcing = lax.dynamic_index_in_dim(forcing_table, selector[0], 0, keepdims=False)
     force_edges = edge_rows(forcing)
-    fits = lax.axis_size("mem") == MEMBERS and lax.axis_size("lat") == 2 and rows % (CHUNKS * PARTS * TILE) == 0
-    if not fits:
-        parents = by_all_to_all(block, ancestors)
-        result = stencil([parents], jnp.zeros(1, jnp.int32), edge_rows(parents), forcing, force_edges)
-        return result.reshape(ensemble.shape)
-
-    def finish(final, starts, forcing, below, above):
-        height = final[0][0].shape[1]
-        own = lax.axis_index("mem").astype(jnp.int32) % PARTS
-        near = (lax.axis_index("lat") == 0).astype(jnp.int32)
-        chosen = jnp.stack([own ^ ((PARTS - 1) * near), (height - TILE) * near])
-        edge = small_call(edge_kernel, 1, (block.shape[0], TILE, block.shape[2]), chosen, final[0], PARTS)[0]
-        pieces = [piece for chunk in final for piece in chunk]
-        return stencil(pieces, jnp.concatenate(starts), swap_edges(edge), forcing, (below, above))
-
-    shared, most, tables, plan = by_crossings(block, ancestors, finish)
-    branches = [functools.partial(plan, rounds) for rounds in range(2, PARTS + 1)]
-    choice = jnp.clip(most[0] - 2, 0, PARTS - 2)
-    result = lax.switch(choice, branches, block, shared, *tables, (forcing, *force_edges))
-    return result.reshape(ensemble.shape)
+    if lax.axis_size("mem") == MEMBERS and lax.axis_size("lat") == 2 and rows % (sum(CHUNKS) * PARTS * TILE) == 0:
+        parents, edge = by_crossings(here, block, ancestors)
+        edges = (edge, edge)
+    else:
+        parents = [by_all_to_all(block, ancestors)]
+        edges = edge_rows(parents[0])
+    return stencil(here, parents, edges, forcing, force_edges).reshape(ensemble.shape)
 
 
 def solution(mesh):

time: 103 us -> 82.4 us (0.80)
  waiting for transfers between devices: 48.9 us -> 35.8 us
  starting transfers between devices: 27.3 us -> 23.3 us
  other arithmetic: 3.6 us -> 0.07 us
  Pallas kernels: 17.5 us -> 20 us
  local copies, waits for them, and re-layouts: 2.94 us -> 0.69 us
    ppermute x18 -> x16, waiting for transfers between devices: 46.8 us -> 32.3 us  [shift(): lax.ppermute(values, 'mem', [(i, i ^ distance) for i in range(MEMBERS)])]
    ppermute x18 -> x16, starting transfers between devices: 25.3 us -> 21.3 us  [shift(): lax.ppermute(values, 'mem', [(i, i ^ distance) for i in range(MEMBERS)])]
    pallas_call x8 -> x9, Pallas kernels: 17.5 us -> 20 us  [the longest x1 10.5 us: stencil(): pl.pallas_call(functools.partial(stencil_kernel, lax.axis_size('lat'), ch...]
    ppermute x2, waiting for transfers between devices: 1.2 us -> 2.58 us  [swap_edges(): got = lax.ppermute(sent, 'lat', [(0, 1), (1, 0)])]
    reduce_sum x4 -> x0, other arithmetic: 1.23 us -> none  [the longest x1 0.84 us: by_crossings(): jnp.sum(jnp.where(slots[:, None] == ids[None, :], ancestors[None, :], 0),...]
  transfers between devices with their start and end apart: 21 -> 19, of which waited for: 12 -> 12; matrix products, arithmetic and copies ran while one was open for 5% -> 0% of each run, Pallas kernels for 4% -> 8%
where the time goes in v2:
time: 82.4 us; the launch traced here: 82.1 us
  waiting for transfers between devices  35.8 us (43%)
  starting transfers between devices  23.3 us (28%)
  Pallas kernels  20 us (24%)
  between operations  2.05 us (2%)
    ppermute x16, waiting for transfers between devices, shift(): lax.ppermute(values, 'mem', [(i, i ^ distance) for i in range(MEMBERS)])  32.3 us
    ppermute x16, starting transfers between devices, shift(): lax.ppermute(values, 'mem', [(i, i ^ distance) for i in range(MEMBERS)])  21.3 us
    pallas_call x1, Pallas kernels, stencil(): pl.pallas_call(functools.partial(stencil_kernel, lax.axis_size('lat'), ch...  10.5 us
    pallas_call x8, Pallas kernels, small_call(): pl.pallas_call(kernel, out_shape=outs, in_specs=[smem] * (1 + len(tables)...  9.51 us
    ppermute x2, waiting for transfers between devices, swap_edges(): got = lax.ppermute(sent, 'lat', [(0, 1), (1, 0)])  2.58 us
    ppermute x1, starting transfers between devices, by_crossings(): lax.ppermute(other, 'groups', [(i, (i + 1) % groups) for i in range(group...  2 us
  transfers between devices with their start and end apart: 19, of which 12 were waited for; matrix products, arithmetic and copies ran while one was open for 0% of the time, Pallas kernels for 8%

profile of v2, /device:TPU:0, one launch (start us, length us, event | category | flops | bytes accessed | tf_op | source)
XLA Modules:
  0.0 82.1 jit_solution(17830346770350387421)
XLA Ops:
  0.1 1.7 %shard_map.46 = (f32[6,16,512]{2,1,0:T(8,128)S(1)}, f32[6,16,512]{2,1,0:T(8,128)S(1)}, f32[6,16,512]{2,1,0:T(8,128)S(1)}) custom-call(s32[2]{0:T(128)S(1)} %pad_add_fusion.here_ref, f32[6,128,512]{2,1,0:T(8,128)} %bitcast.13), custom_call_target="tpu_custom_call" | custom-call | bytes 1179648 | tf_op jit(solution)/shard_map/pallas_call | solution.py:257
  1.8 3.0 %collective-permute-start.49 = (f32[6,16,512]{2,1,0:T(8,128)S(1)}, f32[6,16,512]{2,1,0:T(8,128)S(1)}, u32[]{:S(2)}, u32[]{:S(2)}) collective-permute-start(f32[6,16,512]{2,1,0:T(8,128)S(1)} %get-tuple-element.134.refs_0_), channel_id=1, source_target_pairs={{0,2},{2,0},{4,6},{6,4},{8,10},{10,8},{12,14},{14,12},{1,3},{3,1},... | collective-permute-start | bytes 589832 | tf_op jit(solution)/shard_map/ppermute | solution.py:249
  4.8 1.6 %collective-permute-start.50 = (f32[6,16,512]{2,1,0:T(8,128)S(1)}, f32[6,16,512]{2,1,0:T(8,128)S(1)}, u32[]{:S(2)}, u32[]{:S(2)}) collective-permute-start(f32[6,16,512]{2,1,0:T(8,128)S(1)} %get-tuple-element.137), channel_id=1, source_target_pairs={{0,4},{2,6},{4,0},{6,2},{8,12},{10,14},{12,8},{14,10},{1,5},{3,7},... | collective-permute-start | bytes 589832 | tf_op jit(solution)/shard_map/ppermute | solution.py:249
  8.3 2.0 %collective-permute-start.48 = (s32[1]{0:T(128)}, s32[1]{0:T(128)}, u32[]{:S(2)}, u32[]{:S(2)}) collective-permute-start(s32[1]{0:T(128)} %get-tuple-element.135), channel_id=1, source_target_pairs={{0,16},{16,0},{1,17},{17,1},{2,18},{18,2},{3,19},{19,3},{4,20},{20... | collective-permute-start | bytes 20 | tf_op jit(solution)/shard_map/ppermute | solution.py:373
  13.3 1.9 %collective-permute-done.51 = f32[6,16,512]{2,1,0:T(8,128)S(1)} collective-permute-done((f32[6,16,512]{2,1,0:T(8,128)S(1)}, f32[6,16,512]{2,1,0:T(8,128)S(1)}, u32[]{:S(2)}, u32[]{:S(2)}) %collective-permute-start.51) | collective-permute-done | bytes 196640 | tf_op jit(solution)/shard_map/ppermute | solution.py:249
  15.2 55.1 %conditional.1 = (f32[6,16,512]{2,1,0:T(8,128)}, f32[6,16,512]{2,1,0:T(8,128)}, f32[6,16,512]{2,1,0:T(8,128)}, f32[6,16,512]{2,1,0:T(8,128)}, f32[6,16,512]{2,1,...) conditional(s32[]{:T(128)} %bitcast.3, (s32[2]{0:T(128)S(1)}, ...), branch_computations={%region_0.1_spmd, %region_1.2_spmd, %region_2.3_spmd} | conditional | bytes 27722548 | solution.py:392
  15.2 1.5 %branch_0_fun.6 = (f32[6,16,512]{2,1,0:T(8,128)S(1)}, f32[6,16,512]{2,1,0:T(8,128)S(1)}) custom-call(s32[2]{0:T(128)S(1)} %get-tuple-element.47.here_ref, s32[4]{0:T(128)S(1)} %get-tuple-element.52.chosen_ref, f32[6,16,512]{2,1,0:T(8,128)S(1)} %get-tuple-element.49.refs_0_, f32[6,16,512]{2,1,0:T(8,128)S(1)} %get-tuple-element.50.refs_1_, ...), custom_call_target="tpu_custom_call" | custom-call | bytes 786432 | tf_op jit(solution)/shard_map/cond/branch_0_fun/pallas_call | solution.py:257
  16.7 2.0 %collective-permute-start = (f32[6,16,512]{2,1,0:T(8,128)S(1)}, f32[6,16,512]{2,1,0:T(8,128)S(1)}, u32[]{:S(2)}, u32[]{:S(2)}) collective-permute-start(f32[6,16,512]{2,1,0:T(8,128)S(1)} %get-tuple-element.54.refs_3_), channel_id=1, source_target_pairs={{0,8},{2,10},{4,12},{6,14},{8,0},{10,2},{12,4},{14,6},{1,9},{3,11}... | collective-permute-start | bytes 589832 | tf_op jit(solution)/shard_map/cond/branch_0_fun/ppermute | solution.py:249
  19.4 2.4 %collective-permute-start.5 = (f32[6,16,512]{2,1,0:T(8,128)S(1)}, f32[6,16,512]{2,1,0:T(8,128)S(1)}, u32[]{:S(2)}, u32[]{:S(2)}) collective-permute-start(f32[6,16,512]{2,1,0:T(8,128)S(1)} %get-tuple-element.60), channel_id=1, source_target_pairs={{0,2},{2,0},{4,6},{6,4},{8,10},{10,8},{12,14},{14,12},{1,3},{3,1},... | collective-permute-start | bytes 589832 | tf_op jit(solution)/shard_map/cond/branch_0_fun/ppermute | solution.py:249
  21.8 1.6 %collective-permute-start.6 = (f32[6,16,512]{2,1,0:T(8,128)S(1)}, f32[6,16,512]{2,1,0:T(8,128)S(1)}, u32[]{:S(2)}, u32[]{:S(2)}) collective-permute-start(f32[6,16,512]{2,1,0:T(8,128)S(1)} %get-tuple-element.61), channel_id=1, source_target_pairs={{0,4},{2,6},{4,0},{6,2},{8,12},{10,14},{12,8},{14,10},{1,5},{3,7},... | collective-permute-start | bytes 589832 | tf_op jit(solution)/shard_map/cond/branch_0_fun/ppermute | solution.py:249
  24.0 4.9 %collective-permute-done.refs_3_.refs_4_ = f32[6,16,512]{2,1,0:T(8,128)S(1)} collective-permute-done((f32[6,16,512]{2,1,0:T(8,128)S(1)}, f32[6,16,512]{2,1,0:T(8,128)S(1)}, u32[]{:S(2)}, u32[]{:S(2)}) %collective-permute-start) | collective-permute-done | bytes 196640 | tf_op jit(solution)/shard_map/cond/branch_0_fun/ppermute | solution.py:249
  28.9 6.5 %collective-permute-done.6.refs_1_ = f32[6,16,512]{2,1,0:T(8,128)S(1)} collective-permute-done((f32[6,16,512]{2,1,0:T(8,128)S(1)}, f32[6,16,512]{2,1,0:T(8,128)S(1)}, u32[]{:S(2)}, u32[]{:S(2)}) %collective-permute-start.6) | collective-permute-done | bytes 196640 | tf_op jit(solution)/shard_map/cond/branch_0_fun/ppermute | solution.py:249
  35.4 2.7 %collective-permute-done.7.refs_2_ = f32[6,16,512]{2,1,0:T(8,128)S(1)} collective-permute-done((f32[6,16,512]{2,1,0:T(8,128)S(1)}, f32[6,16,512]{2,1,0:T(8,128)S(1)}, u32[]{:S(2)}, u32[]{:S(2)}) %collective-permute-start.7) | collective-permute-done | bytes 196640 | tf_op jit(solution)/shard_map/cond/branch_0_fun/ppermute | solution.py:249
  39.5 2.3 %collective-permute-start.9 = (f32[6,16,512]{2,1,0:T(8,128)S(1)}, f32[6,16,512]{2,1,0:T(8,128)S(1)}, u32[]{:S(2)}, u32[]{:S(2)}) collective-permute-start(f32[6,16,512]{2,1,0:T(8,128)S(1)} %get-tuple-element.64), channel_id=1, source_target_pairs={{0,8},{2,10},{4,12},{6,14},{8,0},{10,2},{12,4},{14,6},{1,9},{3,11}... | collective-permute-start | bytes 589832 | tf_op jit(solution)/shard_map/cond/branch_0_fun/ppermute | solution.py:249
  41.8 1.5 %branch_0_fun.7 = (f32[6,16,512]{2,1,0:T(8,128)}, f32[6,16,512]{2,1,0:T(8,128)S(1)}, f32[6,16,512]{2,1,0:T(8,128)S(1)}, f32[6,16,512]{2,1,0:T(8,128)S(1)}) custom-call(s32[2]{0:T(128)S(1)} %get-tuple-element.47.here_ref, s32[4]{0:T(128)S(1)} %get-tuple-element.48.chosen_ref, f32[6,16,512]{2,1,0:T(8,128)S(1)} %get-tuple-element.49.refs_0_, ...), custom_call_target="tpu_custom_call" | custom-call | bytes 1572864 | tf_op jit(solution)/shard_map/cond/branch_0_fun/pallas_call | solution.py:257
  43.3 1.6 %collective-permute-start.2 = (f32[6,16,512]{2,1,0:T(8,128)S(1)}, f32[6,16,512]{2,1,0:T(8,128)}, u32[]{:S(2)}, u32[]{:S(2)}) collective-permute-start(f32[6,16,512]{2,1,0:T(8,128)S(1)} %get-tuple-element.57), channel_id=1, source_target_pairs={{0,2},{2,0},{4,6},{6,4},{8,10},{10,8},{12,14},{14,12},{1,3},{3,1},... | collective-permute-start | bytes 589832 | tf_op jit(solution)/shard_map/cond/branch_0_fun/ppermute | solution.py:249
  45.1 1.8 %collective-permute-start.4 = (f32[6,16,512]{2,1,0:T(8,128)S(1)}, f32[6,16,512]{2,1,0:T(8,128)}, u32[]{:S(2)}, u32[]{:S(2)}) collective-permute-start(f32[6,16,512]{2,1,0:T(8,128)S(1)} %get-tuple-element.59), channel_id=1, source_target_pairs={{0,6},{2,4},{4,2},{6,0},{8,14},{10,12},{12,10},{14,8},{1,7},{3,5},... | collective-permute-start | bytes 589832 | tf_op jit(solution)/shard_map/cond/branch_0_fun/ppermute | solution.py:249
  46.9 6.2 %collective-permute-done.8.refs_3_ = f32[6,16,512]{2,1,0:T(8,128)S(1)} collective-permute-done((f32[6,16,512]{2,1,0:T(8,128)S(1)}, f32[6,16,512]{2,1,0:T(8,128)S(1)}, u32[]{:S(2)}, u32[]{:S(2)}) %collective-permute-start.8) | collective-permute-done | bytes 196640 | tf_op jit(solution)/shard_map/cond/branch_0_fun/ppermute | solution.py:249
  53.0 4.1 %collective-permute-done.9.refs_4_ = f32[6,16,512]{2,1,0:T(8,128)S(1)} collective-permute-done((f32[6,16,512]{2,1,0:T(8,128)S(1)}, f32[6,16,512]{2,1,0:T(8,128)S(1)}, u32[]{:S(2)}, u32[]{:S(2)}) %collective-permute-start.9) | collective-permute-done | bytes 196640 | tf_op jit(solution)/shard_map/cond/branch_0_fun/ppermute | solution.py:249
  59.1 2.5 %collective-permute-start.12 = (f32[6,16,512]{2,1,0:T(8,128)S(1)}, f32[6,16,512]{2,1,0:T(8,128)}, u32[]{:S(2)}, u32[]{:S(2)}) collective-permute-start(f32[6,16,512]{2,1,0:T(8,128)S(1)} %get-tuple-element.68), channel_id=1, source_target_pairs={{0,6},{2,4},{4,2},{6,0},{8,14},{10,12},{12,10},{14,8},{1,7},{3,5},... | collective-permute-start | bytes 589832 | tf_op jit(solution)/shard_map/cond/branch_0_fun/ppermute | solution.py:249
  63.4 1.4 %collective-permute-done.13 = f32[6,8,512]{2,1,0:T(8,128)} collective-permute-done((f32[6,8,512]{2,1,0:T(8,128)S(1)}, f32[6,8,512]{2,1,0:T(8,128)}, u32[]{:S(2)}, u32[]{:S(2)}) %collective-permute-start.13) | collective-permute-done | bytes 98336 | tf_op jit(solution)/shard_map/cond/branch_0_fun/ppermute | solution.py:218
  64.8 2.6 %collective-permute-done.10 = f32[6,16,512]{2,1,0:T(8,128)} collective-permute-done((f32[6,16,512]{2,1,0:T(8,128)S(1)}, f32[6,16,512]{2,1,0:T(8,128)}, u32[]{:S(2)}, u32[]{:S(2)}) %collective-permute-start.10) | collective-permute-done | bytes 196640 | tf_op jit(solution)/shard_map/cond/branch_0_fun/ppermute | solution.py:249
  67.4 2.9 %collective-permute-done.12 = f32[6,16,512]{2,1,0:T(8,128)} collective-permute-done((f32[6,16,512]{2,1,0:T(8,128)S(1)}, f32[6,16,512]{2,1,0:T(8,128)}, u32[]{:S(2)}, u32[]{:S(2)}) %collective-permute-start.12) | collective-permute-done | bytes 196640 | tf_op jit(solution)/shard_map/cond/branch_0_fun/ppermute | solution.py:249
  71.5 10.5 %shard_map.48 = f32[6,128,512]{2,1,0:T(8,128)} custom-call(s32[2]{0:T(128)S(1)} %pad_add_fusion.here_ref, f32[6,16,512]{2,1,0:T(8,128)} %get-tuple-element.140.refs_0_, f32[6,16,512]{2,1,0:T(8,128)} %get-tuple-element.141.refs_1_, f32[6,16,512]{2,1,0:T(8,128)} %get-tuple-element.142.refs_2_, f32[6,16,512]{2,1,0:T(8,128)} %get-tuple-element.143.refs_3_, ...), custom_call_target="tpu_custom_call" | custom-call | flops 19660800 | bytes 3407872 | tf_op jit(solution)/shard_map/pallas_call | solution.py:186
  (33 shorter events, 10.7 us)
Async XLA Ops:
  0.0 10.9 %copy-start = (f32[8,128,512]{2,1,0:T(8,128)S(1)}, f32[8,128,512]{2,1,0:T(8,128)}, u32[]{:S(2)}) copy-start(f32[8,128,512]{2,1,0:T(8,128)} %param.8) | copy-start | bytes 6291460
  1.8 11.5 %collective-permute-start.49 = (f32[6,16,512]{2,1,0:T(8,128)S(1)}, f32[6,16,512]{2,1,0:T(8,128)S(1)}, u32[]{:S(2)}, u32[]{:S(2)}) collective-permute-start(f32[6,16,512]{2,1,0:T(8,128)S(1)} %get-tuple-element.134.refs_0_), channel_id=1, source_target_pairs={{0,2},{2,0},{4,6},{6,4},{8,10},{10,8},{12,14},{14,12},{1,3},{3,1},... | collective-permute-start | bytes 589832 | tf_op jit(solution)/shard_map/ppermute | solution.py:249
  4.8 8.4 %collective-permute-start.50 = (f32[6,16,512]{2,1,0:T(8,128)S(1)}, f32[6,16,512]{2,1,0:T(8,128)S(1)}, u32[]{:S(2)}, u32[]{:S(2)}) collective-permute-start(f32[6,16,512]{2,1,0:T(8,128)S(1)} %get-tuple-element.137), channel_id=1, source_target_pairs={{0,4},{2,6},{4,0},{6,2},{8,12},{10,14},{12,8},{14,10},{1,5},{3,7},... | collective-permute-start | bytes 589832 | tf_op jit(solution)/shard_map/ppermute | solution.py:249
  6.4 8.8 %collective-permute-start.51 = (f32[6,16,512]{2,1,0:T(8,128)S(1)}, f32[6,16,512]{2,1,0:T(8,128)S(1)}, u32[]{:S(2)}, u32[]{:S(2)}) collective-permute-start(f32[6,16,512]{2,1,0:T(8,128)S(1)} %get-tuple-element.138), channel_id=1, source_target_pairs={{0,6},{2,4},{4,2},{6,0},{8,14},{10,12},{12,10},{14,8},{1,7},{3,5},... | collective-permute-start | bytes 589832 | tf_op jit(solution)/shard_map/ppermute | solution.py:249
  6.4 0.7 copy-start.1
  8.3 3.6 %collective-permute-start.48 = (s32[1]{0:T(128)}, s32[1]{0:T(128)}, u32[]{:S(2)}, u32[]{:S(2)}) collective-permute-start(s32[1]{0:T(128)} %get-tuple-element.135), channel_id=1, source_target_pairs={{0,16},{16,0},{1,17},{17,1},{2,18},{18,2},{3,19},{19,3},{4,20},{20... | collective-permute-start | bytes 20 | tf_op jit(solution)/shard_map/ppermute | solution.py:373
  15.2 3.5 %copy-start.2 = (f32[6,128,512]{2,1,0:T(8,128)S(1)}, f32[6,128,512]{2,1,0:T(8,128)}, u32[]{:S(2)}) copy-start(f32[6,128,512]{2,1,0:T(8,128)} %get-tuple-element.53.refs_3_.refs_5_.block_ref) | copy-start | bytes 4718596 | tf_op jit(solution)/shard_map/cond
  16.7 12.2 %collective-permute-start = (f32[6,16,512]{2,1,0:T(8,128)S(1)}, f32[6,16,512]{2,1,0:T(8,128)S(1)}, u32[]{:S(2)}, u32[]{:S(2)}) collective-permute-start(f32[6,16,512]{2,1,0:T(8,128)S(1)} %get-tuple-element.54.refs_3_), channel_id=1, source_target_pairs={{0,8},{2,10},{4,12},{6,14},{8,0},{10,2},{12,4},{14,6},{1,9},{3,11}... | collective-permute-start | bytes 589832 | tf_op jit(solution)/shard_map/cond/branch_0_fun/ppermute | solution.py:249
  19.4 9.5 %collective-permute-start.5 = (f32[6,16,512]{2,1,0:T(8,128)S(1)}, f32[6,16,512]{2,1,0:T(8,128)S(1)}, u32[]{:S(2)}, u32[]{:S(2)}) collective-permute-start(f32[6,16,512]{2,1,0:T(8,128)S(1)} %get-tuple-element.60), channel_id=1, source_target_pairs={{0,2},{2,0},{4,6},{6,4},{8,10},{10,8},{12,14},{14,12},{1,3},{3,1},... | collective-permute-start | bytes 589832 | tf_op jit(solution)/shard_map/cond/branch_0_fun/ppermute | solution.py:249
  21.8 13.6 %collective-permute-start.6 = (f32[6,16,512]{2,1,0:T(8,128)S(1)}, f32[6,16,512]{2,1,0:T(8,128)S(1)}, u32[]{:S(2)}, u32[]{:S(2)}) collective-permute-start(f32[6,16,512]{2,1,0:T(8,128)S(1)} %get-tuple-element.61), channel_id=1, source_target_pairs={{0,4},{2,6},{4,0},{6,2},{8,12},{10,14},{12,8},{14,10},{1,5},{3,7},... | collective-permute-start | bytes 589832 | tf_op jit(solution)/shard_map/cond/branch_0_fun/ppermute | solution.py:249
  23.4 14.7 %collective-permute-start.7 = (f32[6,16,512]{2,1,0:T(8,128)S(1)}, f32[6,16,512]{2,1,0:T(8,128)S(1)}, u32[]{:S(2)}, u32[]{:S(2)}) collective-permute-start(f32[6,16,512]{2,1,0:T(8,128)S(1)} %get-tuple-element.62), channel_id=1, source_target_pairs={{0,6},{2,4},{4,2},{6,0},{8,14},{10,12},{12,10},{14,8},{1,7},{3,5},... | collective-permute-start | bytes 589832 | tf_op jit(solution)/shard_map/cond/branch_0_fun/ppermute | solution.py:249
  23.4 18.4 %collective-permute-start.1 = (f32[6,16,512]{2,1,0:T(8,128)S(1)}, f32[6,16,512]{2,1,0:T(8,128)S(1)}, u32[]{:S(2)}, u32[]{:S(2)}) collective-permute-start(f32[6,16,512]{2,1,0:T(8,128)S(1)} %get-tuple-element.55), channel_id=1, source_target_pairs={{0,8},{2,10},{4,12},{6,14},{8,0},{10,2},{12,4},{14,6},{1,9},{3,11}... | collective-permute-start | bytes 589832 | tf_op jit(solution)/shard_map/cond/branch_0_fun/ppermute | solution.py:249
  38.8 14.3 %collective-permute-start.8 = (f32[6,16,512]{2,1,0:T(8,128)S(1)}, f32[6,16,512]{2,1,0:T(8,128)S(1)}, u32[]{:S(2)}, u32[]{:S(2)}) collective-permute-start(f32[6,16,512]{2,1,0:T(8,128)S(1)} %get-tuple-element.63), channel_id=1, source_target_pairs={{0,8},{2,10},{4,12},{6,14},{8,0},{10,2},{12,4},{14,6},{1,9},{3,11}... | collective-permute-start | bytes 589832 | tf_op jit(solution)/shard_map/cond/branch_0_fun/ppermute | solution.py:249
  39.5 17.7 %collective-permute-start.9 = (f32[6,16,512]{2,1,0:T(8,128)S(1)}, f32[6,16,512]{2,1,0:T(8,128)S(1)}, u32[]{:S(2)}, u32[]{:S(2)}) collective-permute-start(f32[6,16,512]{2,1,0:T(8,128)S(1)} %get-tuple-element.64), channel_id=1, source_target_pairs={{0,8},{2,10},{4,12},{6,14},{8,0},{10,2},{12,4},{14,6},{1,9},{3,11}... | collective-permute-start | bytes 589832 | tf_op jit(solution)/shard_map/cond/branch_0_fun/ppermute | solution.py:249
  43.3 15.8 %collective-permute-start.2 = (f32[6,16,512]{2,1,0:T(8,128)S(1)}, f32[6,16,512]{2,1,0:T(8,128)}, u32[]{:S(2)}, u32[]{:S(2)}) collective-permute-start(f32[6,16,512]{2,1,0:T(8,128)S(1)} %get-tuple-element.57), channel_id=1, source_target_pairs={{0,2},{2,0},{4,6},{6,4},{8,10},{10,8},{12,14},{14,12},{1,3},{3,1},... | collective-permute-start | bytes 589832 | tf_op jit(solution)/shard_map/cond/branch_0_fun/ppermute | solution.py:249
  45.0 16.6 %collective-permute-start.3 = (f32[6,16,512]{2,1,0:T(8,128)S(1)}, f32[6,16,512]{2,1,0:T(8,128)}, u32[]{:S(2)}, u32[]{:S(2)}) collective-permute-start(f32[6,16,512]{2,1,0:T(8,128)S(1)} %get-tuple-element.58), channel_id=1, source_target_pairs={{0,4},{2,6},{4,0},{6,2},{8,12},{10,14},{12,8},{14,10},{1,5},{3,7},... | collective-permute-start | bytes 589832 | tf_op jit(solution)/shard_map/cond/branch_0_fun/ppermute | solution.py:249
  45.1 16.9 %collective-permute-start.4 = (f32[6,16,512]{2,1,0:T(8,128)S(1)}, f32[6,16,512]{2,1,0:T(8,128)}, u32[]{:S(2)}, u32[]{:S(2)}) collective-permute-start(f32[6,16,512]{2,1,0:T(8,128)S(1)} %get-tuple-element.59), channel_id=1, source_target_pairs={{0,6},{2,4},{4,2},{6,0},{8,14},{10,12},{12,10},{14,8},{1,7},{3,5},... | collective-permute-start | bytes 589832 | tf_op jit(solution)/shard_map/cond/branch_0_fun/ppermute | solution.py:249
  58.0 9.4 %collective-permute-start.10 = (f32[6,16,512]{2,1,0:T(8,128)S(1)}, f32[6,16,512]{2,1,0:T(8,128)}, u32[]{:S(2)}, u32[]{:S(2)}) collective-permute-start(f32[6,16,512]{2,1,0:T(8,128)S(1)} %get-tuple-element.66), channel_id=1, source_target_pairs={{0,2},{2,0},{4,6},{6,4},{8,10},{10,8},{12,14},{14,12},{1,3},{3,1},... | collective-permute-start | bytes 589832 | tf_op jit(solution)/shard_map/cond/branch_0_fun/ppermute | solution.py:249
  59.1 8.3 %collective-permute-start.11 = (f32[6,16,512]{2,1,0:T(8,128)S(1)}, f32[6,16,512]{2,1,0:T(8,128)}, u32[]{:S(2)}, u32[]{:S(2)}) collective-permute-start(f32[6,16,512]{2,1,0:T(8,128)S(1)} %get-tuple-element.67), channel_id=1, source_target_pairs={{0,4},{2,6},{4,0},{6,2},{8,12},{10,14},{12,8},{14,10},{1,5},{3,7},... | collective-permute-start | bytes 589832 | tf_op jit(solution)/shard_map/cond/branch_0_fun/ppermute | solution.py:249
  59.1 11.2 %collective-permute-start.12 = (f32[6,16,512]{2,1,0:T(8,128)S(1)}, f32[6,16,512]{2,1,0:T(8,128)}, u32[]{:S(2)}, u32[]{:S(2)}) collective-permute-start(f32[6,16,512]{2,1,0:T(8,128)S(1)} %get-tuple-element.68), channel_id=1, source_target_pairs={{0,6},{2,4},{4,2},{6,0},{8,14},{10,12},{12,10},{14,8},{1,7},{3,5},... | collective-permute-start | bytes 589832 | tf_op jit(solution)/shard_map/cond/branch_0_fun/ppermute | solution.py:249
  63.3 1.5 %collective-permute-start.13 = (f32[6,8,512]{2,1,0:T(8,128)S(1)}, f32[6,8,512]{2,1,0:T(8,128)}, u32[]{:S(2)}, u32[]{:S(2)}) collective-permute-start(f32[6,8,512]{2,1,0:T(8,128)S(1)} %branch_0_fun.11), channel_id=1, source_target_pairs={{0,1},{1,0},{2,3},{3,2},{4,5},{5,4},{6,7},{7,6},{8,9},{9,8},{10,11... | collective-permute-start | bytes 294920 | tf_op jit(solution)/shard_map/cond/branch_0_fun/ppermute | solution.py:218
  70.4 1.2 %collective-permute-start.52 = (f32[8,512]{1,0:T(8,128)S(1)}, f32[8,512]{1,0:T(8,128)S(1)}, u32[]{:S(2)}, u32[]{:S(2)}) collective-permute-start(f32[8,512]{1,0:T(8,128)S(1)} %dynamic-slice_bitcast_fusion.1), channel_id=1, source_target_pairs={{0,1},{1,0},{2,3},{3,2},{4,5},{5,4},{6,7},{7,6},{8,9},{9,8},{10,11... | collective-permute-start | bytes 49160 | tf_op jit(solution)/shard_map/ppermute | solution.py:218
